TPU v7x, 512 devices: a whole 4x4x16 slice. The times are simulated.
512 devices in a mesh: layer: 4 (over y), dp: 4 (over x_lo, core), mp: 32 (over z, x_hi).
Axes of the slice: x: 4 (x_hi: 2, x_lo: 2; x = x_hi * 2 + x_lo), y: 4, z: 16, core: 2. Of those that a mesh axis runs over, the one named last changes fastest.
Arguments:
- mlp_in: bfloat16 [4, 128, 2048], P('layer', 'dp', 'mp'), may hold values from -6 to 6
- gate_weight: bfloat16 [4, 2048, 8192], P('layer', None, ('dp', 'mp')), may hold values from -0.125 to 0.125
- up_weight: bfloat16 [4, 2048, 8192], P('layer', None, ('dp', 'mp')), may hold values from -0.125 to 0.125
- down_weight: bfloat16 [4, 8192, 2048], P('layer', ('dp', 'mp')), may hold values from -0.0625 to 0.0625
- enc_weight: bfloat16 [4, 2048, 16384], P('layer', None, ('dp', 'mp')), may hold values from -0.125 to 0.125
- enc_bias: float32 [4, 16384], P('layer', ('dp', 'mp')), may hold values from -3 to 3
- dec_weight: bfloat16 [4, 4, 16384, 2048], P('layer', None, ('dp', 'mp')), may hold values from -0.046875 to 0.046875
Outputs:
- error_nodes: bfloat16 [4, 128, 2048], P('layer', 'dp', 'mp')
- latents: bfloat16 [4, 128, 16384], P('layer', None, ('dp', 'mp'))
All inputs are finite; a program needn't handle non-finite values.
Results may differ from a plain program's by a relative error of at most 0.0049.
Values may be sent and summed in bfloat16 or wider, within the bound.
No kernel may reach another device: no remote copies, remote signals or barrier semaphores. Data moves between devices by JAX's collectives and lax.ppermute only.
A program may use at most 64 MiB of HBM per device.

v0:
```python
import jax
import jax.numpy as jnp
from jax import lax
from jax.sharding import PartitionSpec as P


def choose_source(weights, source, layers):
    return lax.dynamic_index_in_dim(weights, jnp.clip(source, 0, layers - 1), 0, keepdims=False)


def body(mlp_in, gate_weight, up_weight, down_weight, enc_weight, enc_bias, dec_weight):
    layer_now = lax.axis_index("layer")
    layers = lax.axis_size("layer")
    features_full = lax.all_gather(mlp_in, "mp", axis=2, tiled=True)
    tok_rows = features_full.shape[1]
    width = features_full.shape[2]
    gathered = lax.all_gather(features_full.reshape(tok_rows, 1, width), "dp", axis=1, tiled=True)
    spread = gathered.shape[1]
    all_rows = gathered.reshape(tok_rows * spread, width)
    gate_part = jnp.dot(all_rows, gate_weight[0], preferred_element_type=jnp.float32)
    up_part = jnp.dot(all_rows, up_weight[0], preferred_element_type=jnp.float32)
    hidden = (jax.nn.silu(gate_part) * up_part).astype(jnp.bfloat16)
    pre_act = (
        jnp.dot(all_rows, enc_weight[0], preferred_element_type=jnp.float32) + enc_bias[0][None, :]
    )
    latent = jnp.maximum(pre_act, jnp.float32(0.0)).astype(jnp.bfloat16)
    lat_width = latent.shape[1]
    latent_out = (
        latent.reshape(tok_rows, spread, lat_width)
        .transpose(1, 0, 2)
        .reshape(1, tok_rows * spread, lat_width)
    )
    every_layer = lax.all_gather(latent[None], "layer", axis=0, tiled=True)
    keep_mask = (lax.iota(jnp.int32, layers) <= layer_now).astype(jnp.bfloat16)
    stacked = every_layer * keep_mask[:, None, None]
    sources = [which for which in range(layers)]
    latent_cat = jnp.concatenate([stacked[which] for which in range(layers)], axis=1)
    weight_cat = jnp.concatenate(
        [choose_source(dec_weight[0], sources[which], layers) for which in range(layers)], axis=0
    )
    partial_value = jnp.dot(hidden, down_weight[0], preferred_element_type=jnp.float32)
    partial_value = partial_value - jnp.dot(
        latent_cat, weight_cat, preferred_element_type=jnp.float32
    )
    summed = lax.psum_scatter(
        partial_value.reshape(tok_rows, spread * width),
        ("dp", "mp"),
        scatter_dimension=1,
        tiled=True,
    )
    error_out = summed.astype(jnp.bfloat16).reshape(1, tok_rows, -1)
    return (error_out, latent_out)


def solution(mesh):
    return jax.shard_map(
        body,
        mesh=mesh,
        in_specs=(
            P("layer", "dp", "mp"),
            P("layer", None, ("dp", "mp")),
            P("layer", None, ("dp", "mp")),
            P("layer", ("dp", "mp"), None),
            P("layer", None, ("dp", "mp")),
            P("layer", ("dp", "mp")),
            P("layer", None, ("dp", "mp"), None),
        ),
        out_specs=(P("layer", "dp", "mp"), P("layer", None, ("dp", "mp"))),
        check_vma=False,
    )
```

profile of v0, /device:TPU:24, one launch (start us, length us, event | category | flops | bytes accessed | tf_op | source)
XLA Modules:
  0.0 719.7 jit_solution(13167802963294468820)
XLA Ops:
  7.2 0.0 copy-start
  7.2 0.0 copy-start.3
  7.2 0.0 reduce-scatter.4.cloned.1.call-start
  7.3 0.8 copy.15
  8.1 88.1 %all_gather.9 = bf16[1,32,2048]{1,0,2:T(2,128)(2,1)S(1)} all-gather(bf16[1,32,64]{1,0,2:T(2,128)(2,1)S(1)} %copy.15), channel_id=1, replica_groups=mesh['layer'=4,'dp'=4,'mp'=32] {'mp'}, dimensions={2}, use_global_device_ids=true | all-gather | bytes 135168 | tf_op jit(solution)/shard_map/all_gather | solution.py:14
  96.2 0.5 copy.16
  96.7 0.0 copy-start.1
  96.7 0.0 copy-start.2
  96.7 6.6 all-gather
  103.4 0.4 reshape.36
  103.8 1.2 fusion.15
  105.0 0.0 copy-done
  105.1 0.0 copy-done.3
  105.1 0.3 fusion.8
  105.4 12.1 %all-gather.1 = bf16[512,128]{1,0:T(8,128)(2,1)S(1)} all-gather(bf16[128,128]{1,0:T(8,128)(2,1)S(1)} %fusion.8), channel_id=3, replica_groups=mesh['layer'=4,'dp'=4,'mp'=32] {'layer'}, dimensions={0}, use_global_device_ids=true | all-gather | bytes 163840 | tf_op jit(solution)/shard_map/all_gather | solution.py:33
  117.5 0.1 broadcast_multiply_fusion
  117.6 2.7 slice_bitcast_fusion.3
  120.3 0.0 copy-done.1
  120.3 0.0 copy-done.2
  120.3 0.8 fusion.10
  121.2 1.8 convolution_subtract_fusion
  123.0 0.5 reshape.37
  123.5 2.6 copy.18
  126.1 0.0 reduce-scatter.4.cloned.1.call-update
  126.1 0.6 copy.17
  126.8 584.7 %reduce-scatter.4.cloned.1.call-done = f32[64,32]{1,0:T(8,128)} async-done(((f32[8192,32]{1,0:T(8,128)}), f32[64,32]{1,0:T(8,128)}) %reduce-scatter.4.cloned.1.call-update) | async-done | bytes 8208
  711.4 1.4 copy.19
  (2 shorter events, 0.0 us)
Async XLA Ops:
  7.2 97.9 %copy-start = (bf16[1,2048,128]{2,1,0:T(8,128)(2,1)S(1)}, bf16[1,2048,128]{2,1,0:T(8,128)(2,1)}, u32[]{:S(2)}) copy-start(bf16[1,2048,128]{2,1,0:T(8,128)(2,1)} %param.11) | copy-start | bytes 1572868
  7.2 97.9 %copy-start.3 = (f32[1,128]{1,0:T(1,128)S(1)}, f32[1,128]{1,0:T(1,128)}, u32[]{:S(2)}) copy-start(f32[1,128]{1,0:T(1,128)} %param.12) | copy-start | bytes 1540
  7.2 704.2 %reduce-scatter.4.cloned.1.call-start = ((), (), s32[]{:S(2)}) async-start(), calls=%async_computation.1 | async-start | bytes 4227072
  96.7 23.6 %copy-start.1 = (bf16[1,64,2048]{2,1,0:T(8,128)(2,1)S(1)}, bf16[1,64,2048]{2,1,0:T(8,128)(2,1)}, u32[]{:S(2)}) copy-start(bf16[1,64,2048]{2,1,0:T(8,128)(2,1)} %param.10) | copy-start | bytes 786436
  96.7 23.6 %copy-start.2 = (bf16[1,2048,64]{1,2,0:T(8,128)(2,1)S(1)}, bf16[1,2048,64]{1,2,0:T(8,128)(2,1)}, u32[]{:S(2)}) copy-start(bf16[1,2048,64]{1,2,0:T(8,128)(2,1)} %param.9) | copy-start | bytes 786436
Sparse Core Ops, SparseCore 0:
  126.3 585.1 reduce-scatter.3
where the time goes:
time: 725 us; the launch traced here: 720 us
  waiting for transfers between devices  585 us (81%)
  blocking collectives  107 us (15%)
  between operations  14.1 us (2%)
  local copies, waits for them, and re-layouts  9.71 us (1%)
    unnamed x2, waiting for transfers between devices  585 us
    all_gather x1, blocking collectives, body(): features_full = lax.all_gather(mlp_in, 'mp', axis=2, tiled=True)  88.1 us
  transfers between devices with their start and end apart: 1, of which 1 were waited for; matrix products, arithmetic and copies ran while one was open for 0% of the time, Pallas kernels for 0%

commit v1 on v0

v1 whole, which is shorter than its diff:
```python
import jax
import jax.numpy as jnp
from jax import lax
from jax.sharding import Mesh, PartitionSpec as P

DP = ("x_lo", "core")
MP = ("z", "x_hi")


def split_mesh(mesh):
    return Mesh(mesh.devices.reshape(4, 2, 2, 16, 2), ("layer", "x_lo", "core", "z", "x_hi"))


def body(mlp_in, gate_weight, up_weight, down_weight, enc_weight, enc_bias, dec_weight):
    layer_now = lax.axis_index("layer")
    layers = lax.axis_size("layer")
    n_mp = lax.axis_size(MP)
    n_dp = lax.axis_size(DP)
    rows, part = mlp_in.shape[1:]
    width = rows_all = None
    spread = jnp.broadcast_to(mlp_in, (n_mp, rows, part))
    blocks = lax.all_to_all(spread, MP, 0, 0, tiled=True)
    own_rows = blocks.transpose(1, 0, 2).reshape(rows, n_mp * part)
    all_rows = lax.all_gather(own_rows, DP, axis=0, tiled=True)
    tokens, width = all_rows.shape
    gate_part = jnp.dot(all_rows, gate_weight[0], preferred_element_type=jnp.float32)
    up_part = jnp.dot(all_rows, up_weight[0], preferred_element_type=jnp.float32)
    hidden = (jax.nn.silu(gate_part) * up_part).astype(jnp.bfloat16)
    pre_act = (
        jnp.dot(all_rows, enc_weight[0], preferred_element_type=jnp.float32) + enc_bias[0][None, :]
    )
    latent = jnp.maximum(pre_act, jnp.float32(0.0)).astype(jnp.bfloat16)
    every = lax.all_to_all(
        jnp.broadcast_to(latent, (layers,) + latent.shape), "layer", 0, 0, tiled=True
    )
    keep = (lax.iota(jnp.int32, layers) <= layer_now).astype(jnp.bfloat16)
    every = every * keep[:, None, None]
    cat = every.transpose(1, 0, 2).reshape(tokens, -1)
    partial = jnp.dot(hidden, down_weight[0], preferred_element_type=jnp.float32)
    partial = partial - jnp.dot(
        cat, dec_weight[0].reshape(-1, width), preferred_element_type=jnp.float32
    )
    got = lax.all_to_all(
        partial.astype(jnp.bfloat16).reshape(n_dp, rows, width), DP, 0, 0, tiled=True
    )
    mine = got.astype(jnp.float32).sum(0)
    send = mine.astype(jnp.bfloat16).reshape(rows, n_mp, part).transpose(1, 0, 2)
    got = lax.all_to_all(send, MP, 0, 0, tiled=True)
    error = got.astype(jnp.float32).sum(0).astype(jnp.bfloat16)
    return error[None], latent[None]


def solution(mesh):
    return jax.shard_map(
        body,
        mesh=split_mesh(mesh),
        in_specs=(
            P("layer", DP, MP),
            P("layer", None, DP + MP),
            P("layer", None, DP + MP),
            P("layer", DP + MP, None),
            P("layer", None, DP + MP),
            P("layer", DP + MP),
            P("layer", None, DP + MP, None),
        ),
        out_specs=(P("layer", DP, MP), P("layer", None, DP + MP)),
        check_vma=False,
    )
```

time: 725 us -> 92.2 us (0.13)
  waiting for transfers between devices: 585 us -> 18.6 us
  blocking collectives: 107 us -> 38.5 us
  starting transfers between devices: 0.04 us -> 22.6 us
  between operations: 14.1 us -> 0.78 us
    unnamed x2 -> x0, waiting for transfers between devices: 585 us -> none
    all_gather x3 -> x1, blocking collectives: 107 us -> 6.5 us  [body(): all_rows = lax.all_gather(own_rows, DP, axis=0, tiled=True)]
    all_to_all x0 -> x2, blocking collectives: none -> 32 us  [the longest x1 20.8 us: body(): got = lax.all_to_all(send, MP, 0, 0, tiled=True)]
    all_to_all x0 -> x2, starting transfers between devices: none -> 22.6 us  [the longest x1 17.9 us: body(): blocks = lax.all_to_all(spread, MP, 0, 0, tiled=True)]
    all_to_all x0 -> x2, waiting for transfers between devices: none -> 18.6 us  [the longest x1 17.5 us: body(): blocks = lax.all_to_all(spread, MP, 0, 0, tiled=True)]
  transfers between devices with their start and end apart: 1 -> 2, of which waited for: 1 -> 2; matrix products, arithmetic and copies ran while one was open for 0% -> 3% of each run, Pallas kernels for 0% -> 0%
where the time goes in v1:
time: 92.2 us; the launch traced here: 90.9 us
  blocking collectives  38.5 us (42%)
  starting transfers between devices  22.6 us (25%)
  waiting for transfers between devices  18.6 us (20%)
  matrix products  5.75 us (6%)
  local copies, waits for them, and re-layouts  3.88 us (4%)
    all_to_all x1, blocking collectives, body(): got = lax.all_to_all(send, MP, 0, 0, tiled=True)  20.8 us
    all_to_all x1, starting transfers between devices, body(): blocks = lax.all_to_all(spread, MP, 0, 0, tiled=True)  17.9 us
    all_to_all x1, waiting for transfers between devices, body(): blocks = lax.all_to_all(spread, MP, 0, 0, tiled=True)  17.5 us
    all_to_all x1, blocking collectives, body(): lax.all_to_all(partial.astype(jnp.bfloat16).reshape(n_dp, rows, width), D...  11.2 us
    all_gather x1, blocking collectives, body(): all_rows = lax.all_gather(own_rows, DP, axis=0, tiled=True)  6.5 us
    all_to_all x1, starting transfers between devices, body(): lax.all_to_all(jnp.broadcast_to(latent, (layers,) + latent.shape), 'layer...  4.68 us
    dot_general x1, matrix products, body(): jnp.dot(hidden, down_weight[0], preferred_element_type=jnp.float32)  2.86 us
  transfers between devices with their start and end apart: 2, of which 2 were waited for; matrix products, arithmetic and copies ran while one was open for 3% of the time, Pallas kernels for 0%

profile of v1, /device:TPU:24, one launch (start us, length us, event | category | flops | bytes accessed | tf_op | source)
XLA Modules:
  0.0 90.9 jit_solution(17702901810667421857)
XLA Ops:
  0.6 0.0 copy-start
  0.6 0.0 copy-start.2
  0.7 0.0 copy-start.4
  0.7 0.0 copy-start.1
  0.7 0.9 broadcast_in_dim.18
  1.6 0.8 reshape.25
  2.4 17.9 %all-to-all-start = ((bf16[32,2,1024]{2,1,0:T(2,128)(2,1)}), bf16[32,2,1024]{2,1,0:T(2,128)(2,1)S(1)}, u32[]{:S(2)}, u32[]{:S(2)}) async-start(bf16[32,2,1024]{2,1,0:T(2,128)(2,1)} %reshape.25), calls=%async_computation | async-start | bytes 262144 | tf_op jit(solution)/shard_map/all_to_all | solution.py:22
  20.4 17.5 %all-to-all-done = bf16[32,2,1024]{2,1,0:T(2,128)(2,1)S(1)} async-done(((bf16[32,2,1024]{2,1,0:T(2,128)(2,1)}), bf16[32,2,1024]{2,1,0:T(2,128)(2,1)S(1)}, u32[]{:S(2)}, u32[]{:S(2)}) %all-to-all-start) | async-done | bytes 131104 | tf_op jit(solution)/shard_map/all_to_all | solution.py:22
  37.9 0.2 reshape.26
  38.1 0.1 copy.12
  38.2 0.3 reshape.21
  38.5 6.5 %all_gather.3 = bf16[128,2048]{1,0:T(8,128)(2,1)S(1)} all-gather(bf16[32,2048]{1,0:T(8,128)(2,1)S(1)} %reshape.21), channel_id=1, replica_groups=mesh['layer'=4,'x_lo'=2,'core'=2,'z'=16,'x_hi'=2] {'x_lo','core'}, dimensions={0}, use_global_device_ids=true | all-gather | bytes 655360 | tf_op jit(solution)/shard_map/all_gather | solution.py:24
  45.0 0.0 copy-done.2
  45.0 0.9 fusion.9
  45.9 0.0 copy-done.4
  45.9 0.0 copy-done.1
  45.9 0.3 fusion.2
  46.2 0.0 copy-start.3
  46.2 0.1 copy.13
  46.3 0.7 broadcast_in_dim.19
  47.0 4.7 %all-to-all-start.1 = ((bf16[4,128,128]{1,2,0:T(8,128)(2,1)}), bf16[4,128,128]{1,2,0:T(8,128)(2,1)S(1)}, u32[]{:S(2)}, u32[]{:S(2)}) async-start(bf16[4,128,128]{1,2,0:T(8,128)(2,1)} %broadcast_in_dim.19), calls=%async_computation.1 | async-start | bytes 262144 | tf_op jit(solution)/shard_map/all_to_all | solution.py:33
  51.7 2.9 %fusion.4 = f32[128,2048]{1,0:T(8,128)} fusion(bf16[128,2048]{1,0:T(8,128)(2,1)S(1)} %all_gather.3, bf16[1,64,2048]{2,1,0:T(8,128)(2,1)} %param.10, bf16[1,2048,64]{1,2,0:T(8,128)(2,1)} %param.9, f32[128,64]{0,1:T(8,128)} %fusion.9), kind=kOutput, calls=%fused_computation.7 | convolution fusion | flops 67158016 | bytes 2129920 | tf_op jit(solution)/shard_map/dot_general | solution.py:39
  54.5 1.1 %all-to-all-done.1 = bf16[4,128,128]{1,2,0:T(8,128)(2,1)S(1)} async-done(((bf16[4,128,128]{1,2,0:T(8,128)(2,1)}), bf16[4,128,128]{1,2,0:T(8,128)(2,1)S(1)}, u32[]{:S(2)}, u32[]{:S(2)}) %all-to-all-start.1) | async-done | bytes 131104 | tf_op jit(solution)/shard_map/all_to_all | solution.py:33
  55.6 0.1 broadcast_multiply_fusion
  55.7 0.0 copy-done
  55.7 1.7 %fusion = bf16[128,2048]{1,0:T(8,128)(2,1)S(1)} fusion(f32[128,2048]{1,0:T(8,128)} %fusion.4, bf16[128,512]{0,1:T(8,128)(2,1)S(1)} %bitcast.33, bf16[512,2048]{1,0:T(8,128)(2,1)S(1)} %bitcast.29), kind=kOutput, calls=%fused_computation.1 | convolution fusion | flops 268959744 | bytes 3801088 | tf_op jit(solution)/shard_map/dot_general | solution.py:40
  57.4 0.0 copy-done.3
  57.4 11.2 %all_to_all.20 = bf16[4,32,2048]{2,1,0:T(8,128)(2,1)S(1)} all-to-all(bf16[4,32,2048]{2,1,0:T(8,128)(2,1)S(1)} %bitcast.30), channel_id=1, replica_groups=mesh['layer'=4,'x_lo'=2,'core'=2,'z'=16,'x_hi'=2] {'x_lo','core'}, dimensions={0} | all-to-all | bytes 1048576 | tf_op jit(solution)/shard_map/all_to_all | solution.py:43
  68.6 0.1 reduce_sum.24
  68.7 0.2 reshape.24
  68.9 0.1 copy.14
  69.1 0.2 reshape.27
  69.2 20.8 %all_to_all.21 = bf16[32,2,1024]{2,1,0:T(2,128)(2,1)S(1)} all-to-all(bf16[32,2,1024]{2,1,0:T(2,128)(2,1)S(1)} %reshape.27), channel_id=1, replica_groups=mesh['layer'=4,'x_lo'=2,'core'=2,'z'=16,'x_hi'=2] {'z','x_hi'}, dimensions={0} | all-to-all | bytes 262144 | tf_op jit(solution)/shard_map/all_to_all | solution.py:48
  90.0 0.2 reshape.28
  90.3 0.7 reduce_sum.25
  (1 shorter events, 0.0 us)
Async XLA Ops:
  0.6 55.0 %copy-start = (bf16[1,4,128,2048]{3,2,1,0:T(8,128)(2,1)S(1)}, bf16[1,4,128,2048]{3,2,1,0:T(8,128)(2,1)}, u32[]{:S(2)}) copy-start(bf16[1,4,128,2048]{3,2,1,0:T(8,128)(2,1)} %param.13) | copy-start | bytes 6291460
  0.6 44.3 %copy-start.2 = (bf16[1,2048,64]{1,2,0:T(8,128)(2,1)S(1)}, bf16[1,2048,64]{1,2,0:T(8,128)(2,1)}, u32[]{:S(2)}) copy-start(bf16[1,2048,64]{1,2,0:T(8,128)(2,1)} %param.8) | copy-start | bytes 786436
  0.7 45.2 %copy-start.4 = (f32[1,128]{1,0:T(1,128)S(1)}, f32[1,128]{1,0:T(1,128)}, u32[]{:S(2)}) copy-start(f32[1,128]{1,0:T(1,128)} %param.12) | copy-start | bytes 1540
  0.7 45.2 %copy-start.1 = (bf16[1,2048,128]{2,1,0:T(8,128)(2,1)S(1)}, bf16[1,2048,128]{2,1,0:T(8,128)(2,1)}, u32[]{:S(2)}) copy-start(bf16[1,2048,128]{2,1,0:T(8,128)(2,1)} %param.11) | copy-start | bytes 1572868
  2.4 35.5 %all-to-all-start = ((bf16[32,2,1024]{2,1,0:T(2,128)(2,1)}), bf16[32,2,1024]{2,1,0:T(2,128)(2,1)S(1)}, u32[]{:S(2)}, u32[]{:S(2)}) async-start(bf16[32,2,1024]{2,1,0:T(2,128)(2,1)} %reshape.25), calls=%async_computation | async-start | bytes 262144 | tf_op jit(solution)/shard_map/all_to_all | solution.py:22
  46.2 11.2 %copy-start.3 = (bf16[128,128]{1,0:T(8,128)(2,1)}, bf16[128,128]{1,0:T(8,128)(2,1)S(1)}, u32[]{:S(2)}) copy-start(bf16[128,128]{1,0:T(8,128)(2,1)S(1)} %fusion.2) | copy-start | bytes 98308
  47.0 8.6 %all-to-all-start.1 = ((bf16[4,128,128]{1,2,0:T(8,128)(2,1)}), bf16[4,128,128]{1,2,0:T(8,128)(2,1)S(1)}, u32[]{:S(2)}, u32[]{:S(2)}) async-start(bf16[4,128,128]{1,2,0:T(8,128)(2,1)} %broadcast_in_dim.19), calls=%async_computation.1 | async-start | bytes 262144 | tf_op jit(solution)/shard_map/all_to_all | solution.py:33

commit v2 on v1

v2 whole, which is shorter than its diff:
```python
import jax
import jax.numpy as jnp
from jax import lax
from jax.experimental import pallas as pl
from jax.experimental.pallas import tpu as pltpu
from jax.sharding import Mesh, PartitionSpec as P

DP = ("x_lo", "core")
MP = ("z", "x_hi")
X = ("x_hi", "x_lo")
F32 = jnp.float32
BF16 = jnp.bfloat16
VMEM_BYTES = 8 * 2**20
VMEM = pl.BlockSpec(memory_space=pltpu.VMEM)
SMEM = pl.BlockSpec(memory_space=pltpu.SMEM)
ANY = pl.BlockSpec(memory_space=pl.ANY)


def split_mesh(mesh):
    return Mesh(mesh.devices.reshape(4, 2, 2, 16, 2), ("layer", "x_lo", "core", "z", "x_hi"))


def call(kernel, name, outs, specs, scratch, flops, n_bytes, out_specs=VMEM):
    return pl.pallas_call(
        kernel,
        name=name,
        out_shape=outs,
        in_specs=specs,
        out_specs=out_specs,
        scratch_shapes=scratch,
        cost_estimate=pl.CostEstimate(flops=flops, bytes_accessed=n_bytes, transcendentals=0),
        compiler_params=pltpu.CompilerParams(vmem_limit_bytes=VMEM_BYTES),
    )


def far(weight):
    return pltpu.with_memory_space_constraint(weight, pltpu.HBM)


def dot(a, b):
    return lax.dot_general(a, b, (((1,), (0,)), ((), ())), preferred_element_type=F32)


def dot_t(a, b):
    return lax.dot_general(a, b, (((1,), (1,)), ((), ())), preferred_element_type=F32)


def low_half(shape):
    return lax.broadcasted_iota(jnp.int32, shape, 1) < shape[1] // 2


def start_all(sems, pairs):
    copies = []
    for i, (source, target) in enumerate(pairs):
        copies.append(pltpu.make_async_copy(source, target, sems.at[i]))
        copies[-1].start()
    return copies


def wait_all(copies):
    for copy in copies:
        copy.wait()


def encode_kernel(got, bias, enc, x, latent, copies, weight, sems):
    n_core, n_hi, n_lo, n_z, half, lanes = got.shape
    loads = start_all(sems, [(enc, weight)])
    low = low_half((half, lanes))
    for lo in range(n_lo):
        for core in range(n_core):
            row = (lo * n_core + core) * 2 * half
            for z in range(n_z):
                a = got[core, 0, lo, z].astype(F32)
                b = got[core, 1, lo, z].astype(F32)
                top = jnp.where(low, a, pltpu.roll(b, lanes // 2, 1))
                bottom = jnp.where(low, pltpu.roll(a, lanes // 2, 1), b)
                cols = slice(z * lanes, (z + 1) * lanes)
                x[row : row + half, cols] = top.astype(BF16)
                x[row + half : row + 2 * half, cols] = bottom.astype(BF16)
    wait_all(loads)
    pre = dot(x[...], weight[...]) + bias[...]
    value = jnp.maximum(pre, F32(0.0)).astype(BF16)
    latent[...] = value
    for s in range(copies.shape[0]):
        copies[s] = value


def hidden_kernel(layer, x, latent, gate, up, down, dec, out, gates, ups, downs, decs, sems):
    loads = start_all(
        sems, [(gate, gates), (up, ups), (down, downs), (dec.at[layer[0]], decs)]
    )
    rows = x[...]
    wait_all(loads[:2])
    gate_part = dot_t(rows, gates[...])
    up_part = dot_t(rows, ups[...])
    hidden = (gate_part / (1.0 + jnp.exp(-gate_part)) * up_part).astype(BF16)
    wait_all(loads[2:])
    tile = 256
    for n in range(0, x.shape[1], tile):
        value = dot(hidden, downs[:, n : n + tile])
        out[:, n : n + tile] = value - dot(latent[...], decs[:, n : n + tile])


def decode_kernel(place, got, partial, dec, keep, give, total, decs, sems):
    n_src = got.shape[0]
    layer, core = place[0], place[1]

    def load(back):
        return pltpu.make_async_copy(dec.at[layer - back], decs.at[back - 1], sems.at[back - 1])

    for back in range(1, n_src):

        @pl.when(layer >= back)
        def _():
            load(back).start()

    total[...] = partial[...]
    tile = 256
    for back in range(1, n_src):

        @pl.when(layer >= back)
        def _():
            load(back).wait()
            rows = got[layer - back]
            for n in range(0, total.shape[1], tile):
                total[:, n : n + tile] = total[:, n : n + tile] - dot(
                    rows, decs[back - 1, :, n : n + tile]
                )

    rows = keep.shape[0] // 2
    for lo in range(2):
        mine = pl.multiple_of((2 * lo + core) * rows, rows)
        theirs = pl.multiple_of((2 * lo + 1 - core) * rows, rows)
        keep[lo * rows : (lo + 1) * rows] = total[pl.ds(mine, rows)]
        give[lo * rows : (lo + 1) * rows] = total[pl.ds(theirs, rows)].astype(BF16)


def join_kernel(place, keep, got, out):
    n_hi, n_lo, n_z, half, lanes = out.shape
    other = 1 - place[1]
    low = low_half((half, lanes))
    for lo in range(n_lo):
        row = lo * 2 * half
        for z in range(n_z):
            cols = slice(z * lanes, (z + 1) * lanes)
            value = keep[row : row + 2 * half, cols] + got[other, row : row + 2 * half, cols].astype(F32)
            top, bottom = value[:half], value[half:]
            out[0, lo, z] = jnp.where(low, top, pltpu.roll(bottom, lanes // 2, 1)).astype(BF16)
            out[1, lo, z] = jnp.where(low, pltpu.roll(top, lanes // 2, 1), bottom).astype(BF16)


def last_kernel(got, out):
    half, lanes = got.shape[1:]
    total = got[0].astype(F32)
    for z in range(1, got.shape[0]):
        total = total + got[z].astype(F32)
    out[0:half] = total[:, 0 : lanes // 2].astype(BF16)
    out[half : 2 * half] = pltpu.roll(total, lanes // 2, 1)[:, 0 : lanes // 2].astype(BF16)


def body(mlp_in, gate_weight, up_weight, down_weight, enc_weight, enc_bias, dec_weight):
    place = jnp.stack([lax.axis_index("layer"), lax.axis_index("core")]).astype(jnp.int32)
    layers, n_core = lax.axis_size("layer"), lax.axis_size("core")
    n_z, n_hi, n_lo = lax.axis_size("z"), lax.axis_size("x_hi"), lax.axis_size("x_lo")
    rows, part = mlp_in.shape[1:]
    half, tokens = rows // 2, rows * n_lo * n_core
    gate, up, down = far(gate_weight[0].T), far(up_weight[0].T), far(down_weight[0])
    enc, dec = far(enc_weight[0]), far(dec_weight[0])
    width, lat = enc.shape
    n_ff = gate.shape[0]
    dma = pltpu.SemaphoreType.DMA
    with jax.named_scope("gather_z"):
        block = jnp.concatenate([mlp_in[0, :half], mlp_in[0, half:]], axis=1)
        spread = jnp.broadcast_to(block, (n_z, half, 2 * part))
        spread, place = lax.optimization_barrier((spread, place))
        got = lax.all_to_all(spread, "z", 0, 0, tiled=True)
    with jax.named_scope("gather_x"):
        got = lax.all_to_all(jnp.broadcast_to(got, (n_hi * n_lo,) + got.shape), X, 0, 0, tiled=True)
    with jax.named_scope("gather_core"):
        got = lax.all_gather(got, "core", axis=0, tiled=False)
        got = got.reshape(n_core, n_hi, n_lo, n_z, half, 2 * part)
    with jax.named_scope("encode"):
        x, latent, copies = call(
            encode_kernel,
            "encode",
            (
                jax.ShapeDtypeStruct((tokens, width), BF16),
                jax.ShapeDtypeStruct((tokens, lat), BF16),
                jax.ShapeDtypeStruct((layers, tokens, lat), BF16),
            ),
            [VMEM, VMEM, ANY],
            [pltpu.VMEM((width, lat), BF16), dma((1,))],
            2 * tokens * width * lat,
            2 * width * lat,
            (VMEM, VMEM, VMEM),
        )(got, enc_bias, enc)
    with jax.named_scope("exchange"):
        every = lax.all_to_all(copies, "layer", 0, 0, tiled=True)
    with jax.named_scope("hidden"):
        partial = call(
            hidden_kernel,
            "hidden",
            jax.ShapeDtypeStruct((tokens, width), F32),
            [SMEM, VMEM, VMEM] + [ANY] * 4,
            [pltpu.VMEM((n_ff, width), BF16) for _ in range(3)]
            + [pltpu.VMEM((lat, width), BF16), dma((4,))],
            6 * tokens * width * n_ff + 2 * tokens * width * lat,
            6 * n_ff * width + 2 * lat * width,
        )(place, x, latent, gate, up, down, dec)
    with jax.named_scope("decode"):
        half_sum = (tokens // n_core, width)
        keep, give = call(
            decode_kernel,
            "decode",
            (jax.ShapeDtypeStruct(half_sum, F32), jax.ShapeDtypeStruct(half_sum, BF16)),
            [SMEM, VMEM, VMEM, ANY],
            [
                pltpu.VMEM((tokens, width), F32),
                pltpu.VMEM((layers - 1, lat, width), BF16),
                dma((layers - 1,)),
            ],
            6 * tokens * width * lat,
            6 * lat * width,
            (VMEM, VMEM),
        )(place, every, partial, dec)
    with jax.named_scope("reduce_core"):
        got = lax.all_gather(give, "core", axis=0, tiled=False)
        send = call(
            join_kernel,
            "join",
            jax.ShapeDtypeStruct((n_hi, n_lo, n_z, half, 2 * part), BF16),
            [SMEM, VMEM, VMEM],
            [],
            0,
            8 * tokens * width,
        )(place, keep, got)
    with jax.named_scope("reduce_x"):
        got = lax.all_to_all(send.reshape(n_hi * n_lo, n_z, half, 2 * part), X, 0, 0, tiled=True)
        send = got.astype(F32).sum(0).astype(BF16)
    with jax.named_scope("reduce_z"):
        got = lax.all_to_all(send, "z", 0, 0, tiled=True)
    with jax.named_scope("last"):
        error = call(
            last_kernel,
            "last",
            jax.ShapeDtypeStruct((rows, part), BF16),
            [VMEM],
            [],
            0,
            2 * n_z * rows * part,
        )(got)
    return error[None], latent[None]


def solution(mesh):
    return jax.shard_map(
        body,
        mesh=split_mesh(mesh),
        in_specs=(
            P("layer", DP, MP),
            P("layer", None, DP + MP),
            P("layer", None, DP + MP),
            P("layer", DP + MP, None),
            P("layer", None, DP + MP),
            P("layer", DP + MP),
            P("layer", None, DP + MP, None),
        ),
        out_specs=(P("layer", DP, MP), P("layer", None, DP + MP)),
        check_vma=False,
    )
```

time: 92.2 us -> 85.8 us (0.931)
  blocking collectives: 38.5 us -> 68.1 us
  waiting for transfers between devices: 18.6 us -> 0.68 us
  starting transfers between devices: 22.6 us -> 4.7 us
  Pallas kernels: 0 us -> 8.37 us
  matrix products: 5.75 us -> 0 us
  local copies, waits for them, and re-layouts: 3.88 us -> 2.17 us
    all_to_all x2 -> x4, blocking collectives: 32 us -> 63.8 us  [the longest x1 27.7 us: body(): got = lax.all_to_all(spread, 'z', 0, 0, tiled=True)]
    all_to_all x2 -> x1, starting transfers between devices: 22.6 us -> 4.7 us  [body(): every = lax.all_to_all(copies, 'layer', 0, 0, tiled=True)]
    all_to_all x2 -> x1, waiting for transfers between devices: 18.6 us -> 0.68 us  [body(): every = lax.all_to_all(copies, 'layer', 0, 0, tiled=True)]
    pallas_call x0 -> x5, Pallas kernels: none -> 8.37 us  [the longest x1 2.53 us: body(): call(decode_kernel, 'decode', (jax.ShapeDtypeStruct(half_sum, F32), jax.S...]
    dot_general x4 -> x0, matrix products: 5.75 us -> none  [the longest x1 2.86 us: body(): jnp.dot(hidden, down_weight[0], preferred_element_type=jnp.float32)]
    all_gather x1 -> x2, blocking collectives: 6.5 us -> 4.35 us  [the longest x1 2.18 us: body(): got = lax.all_gather(give, 'core', axis=0, tiled=False)]
    broadcast_in_dim x2, local copies, waits for them, and re-layouts: 1.56 us -> 0.05 us  [the longest x1 0.03 us: body(): jnp.broadcast_to(got, (n_hi * n_lo,) + got.shape)]
  transfers between devices with their start and end apart: 2 -> 1, of which waited for: 2 -> 1; matrix products, arithmetic and copies ran while one was open for 3% -> 0% of each run, Pallas kernels for 0% -> 3%
where the time goes in v2:
time: 85.8 us; the launch traced here: 84.9 us
  blocking collectives  68.1 us (79%)
  Pallas kernels  8.37 us (10%)
  starting transfers between devices  4.7 us (5%)
  local copies, waits for them, and re-layouts  2.17 us (3%)
    all_to_all x1, blocking collectives, body(): got = lax.all_to_all(spread, 'z', 0, 0, tiled=True)  27.7 us
    all_to_all x1, blocking collectives, body(): got = lax.all_to_all(send, 'z', 0, 0, tiled=True)  15.7 us
    all_to_all x1, blocking collectives, body(): lax.all_to_all(jnp.broadcast_to(got, (n_hi * n_lo,) + got.shape), X, 0, 0...  10.8 us
    all_to_all x1, blocking collectives, body(): lax.all_to_all(send.reshape(n_hi * n_lo, n_z, half, 2 * part), X, 0, 0, t...  9.64 us
    all_to_all x1, starting transfers between devices, body(): every = lax.all_to_all(copies, 'layer', 0, 0, tiled=True)  4.7 us
    pallas_call x1, Pallas kernels, body(): call(decode_kernel, 'decode', (jax.ShapeDtypeStruct(half_sum, F32), jax.S...  2.53 us
    pallas_call x1, Pallas kernels, body(): call(hidden_kernel, 'hidden', jax.ShapeDtypeStruct((tokens, width), F32),...  2.46 us
    all_gather x1, blocking collectives, body(): got = lax.all_gather(give, 'core', axis=0, tiled=False)  2.18 us
  transfers between devices with their start and end apart: 1, of which 1 were waited for; matrix products, arithmetic and copies ran while one was open for 0% of the time, Pallas kernels for 3%

profile of v2, /device:TPU:24, one launch (start us, length us, event | category | flops | bytes accessed | tf_op | source)
XLA Modules:
  0.0 84.9 jit_solution(5900432219078796774)
XLA Ops:
  0.6 0.7 slice_bitcast_fusion.1
  1.3 0.1 pad_add_fusion.layer.place
  1.4 0.1 pad_maximum_fusion
  1.5 27.7 %all_to_all.25 = bf16[16,16,128]{2,1,0:T(8,128)(2,1)S(1)} all-to-all(bf16[16,16,128]{2,1,0:T(8,128)(2,1)S(1)} %broadcast_in_dim.12), channel_id=1, replica_groups=mesh['layer'=4,'x_lo'=2,'core'=2,'z'=16,'x_hi'=2] {'z'}, dimensions={0} | all-to-all | bytes 131072 | tf_op jit(solution)/shard_map/gather_z/all_to_all | solution.py:176
  29.3 10.8 %all_to_all.26 = bf16[4,16,16,128]{3,2,1,0:T(8,128)(2,1)S(1)} all-to-all(bf16[4,16,16,128]{3,2,1,0:T(8,128)(2,1)S(1)} %broadcast_in_dim.13), channel_id=1, replica_groups=mesh['layer'=4,'x_lo'=2,'core'=2,'z'=16,'x_hi'=2] {'x_hi','x_lo'}, dimensions={0} | all-to-all | bytes 524288 | tf_op jit(solution)/shard_map/gather_x/all_to_all | solution.py:178
  40.0 2.2 %all-gather = bf16[8,16,16,128]{3,2,1,0:T(8,128)(2,1)S(1)} all-gather(bf16[4,16,16,128]{3,2,1,0:T(8,128)(2,1)S(1)} %all_to_all.26), channel_id=2, replica_groups=mesh['layer'=4,'x_lo'=2,'core'=2,'z'=16,'x_hi'=2] {'core'}, dimensions={0}, use_global_device_ids=true | all-gather | bytes 786432 | tf_op jit(solution)/shard_map/gather_core/all_gather | solution.py:180
  42.2 0.0 copy-start.1
  42.2 0.7 copy-done.1
  42.9 2.0 %encode.1 = (bf16[128,2048]{1,0:T(8,128)(2,1)S(1)}, bf16[128,128]{1,0:T(8,128)(2,1)}, bf16[4,128,128]{2,1,0:T(8,128)(2,1)}) custom-call(bf16[2,2,2,16,16,128]{5,4,3,2,1,0:T(8,128)(2,1)S(1)} %bitcast.21, f32[1,128]{1,0:T(1,128)S(1)} %copy-done.1, bf16[2048,128]{1,0:T(8,128)(2,1)} %bitcast.26), custom_call_target="tpu_custom_call" | custom-call | flops 67108864 | bytes 524288 | tf_op jit(solution)/shard_map/encode/encode/pallas_call | solution.py:183
  44.9 4.7 %all-to-all-start.2 = ((bf16[4,128,128]{2,1,0:T(8,128)(2,1)}), bf16[4,128,128]{2,1,0:T(8,128)(2,1)S(1)}, u32[]{:S(2)}, u32[]{:S(2)}) async-start(bf16[4,128,128]{2,1,0:T(8,128)(2,1)} %get-tuple-element.11), calls=%async_computation.2 | async-start | bytes 262144 | tf_op jit(solution)/shard_map/exchange/all_to_all | solution.py:198
  49.6 0.0 copy-start
  49.6 0.8 copy-done
  50.3 2.5 %hidden.1.partial = f32[128,2048]{1,0:T(8,128)S(1)} custom-call(s32[2]{0:T(128)S(1)} %pad_add_fusion.layer.place, bf16[128,2048]{1,0:T(8,128)(2,1)S(1)} %get-tuple-element.12.x, bf16[128,128]{1,0:T(8,128)(2,1)S(1)} %copy-done, bf16[64,2048]{1,0:T(8,128)(2,1)} %bitcast.27, bf16[64,2048]{1,0:T(8,128)(2,1)} %bitcast.28, bf16[64,2048]{1,0:T(8,128)(2,1)} %bitcast.29, ...), custom_call_target="tpu_custom_call" | custom-call | flops 167772160 | bytes 1310720 | tf_op jit(solution)/shard_map/hidden/hidden/pallas_call | solution.py:200
  52.8 0.7 all-to-all-done.2.got
  53.5 2.5 %decode.1 = (f32[64,2048]{1,0:T(8,128)S(1)}, bf16[64,2048]{1,0:T(8,128)(2,1)S(1)}) custom-call(s32[2]{0:T(128)S(1)} %pad_add_fusion.layer.place, bf16[4,128,128]{2,1,0:T(8,128)(2,1)S(1)} %all-to-all-done.2.got, f32[128,2048]{1,0:T(8,128)S(1)} %hidden.1.partial, bf16[4,128,2048]{2,1,0:T(8,128)(2,1)} %bitcast.25), custom_call_target="tpu_custom_call" | custom-call | flops 201326592 | bytes 1572864 | tf_op jit(solution)/shard_map/decode/decode/pallas_call | solution.py:212
  56.0 2.2 %all-gather.1 = bf16[128,2048]{1,0:T(8,128)(2,1)S(1)} all-gather(bf16[64,2048]{1,0:T(8,128)(2,1)S(1)} %get-tuple-element.15), channel_id=3, replica_groups=mesh['layer'=4,'x_lo'=2,'core'=2,'z'=16,'x_hi'=2] {'core'}, dimensions={0}, use_global_device_ids=true | all-gather | bytes 786432 | tf_op jit(solution)/shard_map/reduce_core/all_gather | solution.py:227
  58.2 0.7 join.1
  58.9 9.6 %all_to_all.27 = bf16[4,16,16,128]{3,2,1,0:T(8,128)(2,1)S(1)} all-to-all(bf16[4,16,16,128]{3,2,1,0:T(8,128)(2,1)S(1)} %bitcast.22), channel_id=1, replica_groups=mesh['layer'=4,'x_lo'=2,'core'=2,'z'=16,'x_hi'=2] {'x_hi','x_lo'}, dimensions={0} | all-to-all | bytes 524288 | tf_op jit(solution)/shard_map/reduce_x/all_to_all | solution.py:238
  68.6 15.7 %all_to_all.28.got = bf16[16,16,128]{2,1,0:T(8,128)(2,1)S(1)} all-to-all(bf16[16,16,128]{2,1,0:T(8,128)(2,1)S(1)} %reduce_sum.12), channel_id=1, replica_groups=mesh['layer'=4,'x_lo'=2,'core'=2,'z'=16,'x_hi'=2] {'z'}, dimensions={0} | all-to-all | bytes 131072 | tf_op jit(solution)/shard_map/reduce_z/all_to_all | solution.py:241
  84.2 0.7 last.1
  (3 shorter events, 0.1 us)
Async XLA Ops:
  42.2 0.7 copy-start.1
  44.9 8.6 %all-to-all-start.2 = ((bf16[4,128,128]{2,1,0:T(8,128)(2,1)}), bf16[4,128,128]{2,1,0:T(8,128)(2,1)S(1)}, u32[]{:S(2)}, u32[]{:S(2)}) async-start(bf16[4,128,128]{2,1,0:T(8,128)(2,1)} %get-tuple-element.11), calls=%async_computation.2 | async-start | bytes 262144 | tf_op jit(solution)/shard_map/exchange/all_to_all | solution.py:198
  49.6 0.8 copy-start

commit v3 on v2

--- a/solution.py
+++ b/solution.py
@@ -49,6 +49,10 @@
     return lax.broadcasted_iota(jnp.int32, shape, 1) < shape[1] // 2
 
 
+def turn(z, n_z):
+    return (z + n_z // 2) % n_z
+
+
 def start_all(sems, pairs):
     copies = []
     for i, (source, target) in enumerate(pairs):
@@ -62,43 +66,50 @@
         copy.wait()
 
 
-def encode_kernel(got, bias, enc, x, latent, copies, weight, sems):
+def front_kernel(
+    place, got, enc, bias, gate, up, down, dec, latent, copies, out, x, encs, shift, gates, ups, downs, decs, sems
+):
     n_core, n_hi, n_lo, n_z, half, lanes = got.shape
-    loads = start_all(sems, [(enc, weight)])
+    loads = start_all(
+        sems,
+        [
+            (enc, encs),
+            (bias, shift),
+            (gate, gates),
+            (up, ups),
+            (down, downs),
+            (dec.at[place[0]], decs),
+        ],
+    )
     low = low_half((half, lanes))
     for lo in range(n_lo):
         for core in range(n_core):
             row = (lo * n_core + core) * 2 * half
             for z in range(n_z):
-                a = got[core, 0, lo, z].astype(F32)
-                b = got[core, 1, lo, z].astype(F32)
+                at = turn(z, n_z)
+                a = got[core, 0, lo, at].astype(F32)
+                b = got[core, 1, lo, at].astype(F32)
                 top = jnp.where(low, a, pltpu.roll(b, lanes // 2, 1))
                 bottom = jnp.where(low, pltpu.roll(a, lanes // 2, 1), b)
                 cols = slice(z * lanes, (z + 1) * lanes)
                 x[row : row + half, cols] = top.astype(BF16)
                 x[row + half : row + 2 * half, cols] = bottom.astype(BF16)
-    wait_all(loads)
-    pre = dot(x[...], weight[...]) + bias[...]
+    rows = x[...]
+    wait_all(loads[:2])
+    pre = dot(rows, encs[...]) + shift[...]
     value = jnp.maximum(pre, F32(0.0)).astype(BF16)
     latent[...] = value
     for s in range(copies.shape[0]):
         copies[s] = value
-
-
-def hidden_kernel(layer, x, latent, gate, up, down, dec, out, gates, ups, downs, decs, sems):
-    loads = start_all(
-        sems, [(gate, gates), (up, ups), (down, downs), (dec.at[layer[0]], decs)]
-    )
-    rows = x[...]
-    wait_all(loads[:2])
+    wait_all(loads[2:4])
     gate_part = dot_t(rows, gates[...])
     up_part = dot_t(rows, ups[...])
     hidden = (gate_part / (1.0 + jnp.exp(-gate_part)) * up_part).astype(BF16)
-    wait_all(loads[2:])
+    wait_all(loads[4:])
     tile = 256
     for n in range(0, x.shape[1], tile):
-        value = dot(hidden, downs[:, n : n + tile])
-        out[:, n : n + tile] = value - dot(latent[...], decs[:, n : n + tile])
+        cols = slice(n, n + tile)
+        out[:, cols] = dot(hidden, downs[:, cols]) - dot(value, decs[:, cols])
 
 
 def decode_kernel(place, got, partial, dec, keep, give, total, decs, sems):
@@ -145,8 +156,9 @@
             cols = slice(z * lanes, (z + 1) * lanes)
             value = keep[row : row + 2 * half, cols] + got[other, row : row + 2 * half, cols].astype(F32)
             top, bottom = value[:half], value[half:]
-            out[0, lo, z] = jnp.where(low, top, pltpu.roll(bottom, lanes // 2, 1)).astype(BF16)
-            out[1, lo, z] = jnp.where(low, pltpu.roll(top, lanes // 2, 1), bottom).astype(BF16)
+            at = turn(z, n_z)
+            out[0, lo, at] = jnp.where(low, top, pltpu.roll(bottom, lanes // 2, 1)).astype(BF16)
+            out[1, lo, at] = jnp.where(low, pltpu.roll(top, lanes // 2, 1), bottom).astype(BF16)
 
 
 def last_kernel(got, out):
@@ -173,40 +185,32 @@
         block = jnp.concatenate([mlp_in[0, :half], mlp_in[0, half:]], axis=1)
         spread = jnp.broadcast_to(block, (n_z, half, 2 * part))
         spread, place = lax.optimization_barrier((spread, place))
-        got = lax.all_to_all(spread, "z", 0, 0, tiled=True)
+        turned = [[turn(z, n_z) for z in range(n_z)]]
+        got = lax.all_to_all(spread, "z", 0, 0, axis_index_groups=turned, tiled=True)
     with jax.named_scope("gather_x"):
         got = lax.all_to_all(jnp.broadcast_to(got, (n_hi * n_lo,) + got.shape), X, 0, 0, tiled=True)
     with jax.named_scope("gather_core"):
         got = lax.all_gather(got, "core", axis=0, tiled=False)
         got = got.reshape(n_core, n_hi, n_lo, n_z, half, 2 * part)
-    with jax.named_scope("encode"):
-        x, latent, copies = call(
-            encode_kernel,
-            "encode",
+    with jax.named_scope("front"):
+        latent, copies, partial = call(
+            front_kernel,
+            "front",
             (
-                jax.ShapeDtypeStruct((tokens, width), BF16),
                 jax.ShapeDtypeStruct((tokens, lat), BF16),
                 jax.ShapeDtypeStruct((layers, tokens, lat), BF16),
+                jax.ShapeDtypeStruct((tokens, width), F32),
             ),
-            [VMEM, VMEM, ANY],
-            [pltpu.VMEM((width, lat), BF16), dma((1,))],
-            2 * tokens * width * lat,
-            2 * width * lat,
+            [SMEM, VMEM] + [ANY] * 6,
+            [pltpu.VMEM((tokens, width), BF16), pltpu.VMEM((width, lat), BF16), pltpu.VMEM((1, lat), F32)]
+            + [pltpu.VMEM((n_ff, width), BF16) for _ in range(3)]
+            + [pltpu.VMEM((lat, width), BF16), dma((6,))],
+            6 * tokens * width * n_ff + 4 * tokens * width * lat,
+            6 * n_ff * width + 4 * lat * width,
             (VMEM, VMEM, VMEM),
-        )(got, enc_bias, enc)
+        )(place, got, enc, far(enc_bias), gate, up, down, dec)
     with jax.named_scope("exchange"):
         every = lax.all_to_all(copies, "layer", 0, 0, tiled=True)
-    with jax.named_scope("hidden"):
-        partial = call(
-            hidden_kernel,
-            "hidden",
-            jax.ShapeDtypeStruct((tokens, width), F32),
-            [SMEM, VMEM, VMEM] + [ANY] * 4,
-            [pltpu.VMEM((n_ff, width), BF16) for _ in range(3)]
-            + [pltpu.VMEM((lat, width), BF16), dma((4,))],
-            6 * tokens * width * n_ff + 2 * tokens * width * lat,
-            6 * n_ff * width + 2 * lat * width,
-        )(place, x, latent, gate, up, down, dec)
     with jax.named_scope("decode"):
         half_sum = (tokens // n_core, width)
         keep, give = call(
@@ -238,7 +242,7 @@
         got = lax.all_to_all(send.reshape(n_hi * n_lo, n_z, half, 2 * part), X, 0, 0, tiled=True)
         send = got.astype(F32).sum(0).astype(BF16)
     with jax.named_scope("reduce_z"):
-        got = lax.all_to_all(send, "z", 0, 0, tiled=True)
+        got = lax.all_to_all(send, "z", 0, 0, axis_index_groups=turned, tiled=True)
     with jax.named_scope("last"):
         error = call(
             last_kernel,

time: 85.8 us -> 80.2 us (0.935)
  starting transfers between devices: 4.7 us -> 0 us
  blocking collectives: 68.1 us -> 71 us
  Pallas kernels: 8.37 us -> 6.89 us
  local copies, waits for them, and re-layouts: 2.17 us -> 0.75 us
    all_to_all x1 -> x0, starting transfers between devices: 4.7 us -> none  [body(): every = lax.all_to_all(copies, 'layer', 0, 0, tiled=True)]
    all_to_all x2 -> x3, blocking collectives: 43.4 us -> 46.3 us  [the longest x1 22.4 us: body(): lax.all_to_all(spread, 'z', 0, 0, axis_index_groups=turned, tiled=True)]
    pallas_call x2 -> x1, Pallas kernels: 4.48 us -> 2.99 us  [body(): call(front_kernel, 'front', (jax.ShapeDtypeStruct((tokens, lat), BF16), j...]
    unnamed x4 -> x0, local copies, waits for them, and re-layouts: 1.41 us -> none
  transfers between devices with their start and end apart: 1 -> 0, of which waited for: 1 -> 0; matrix products, arithmetic and copies ran while one was open for 0% -> 0% of each run, Pallas kernels for 3% -> 0%
where the time goes in v3:
time: 80.2 us; the launch traced here: 79.5 us
  blocking collectives  71 us (89%)
  Pallas kernels  6.89 us (9%)
    all_to_all x1, blocking collectives, body(): lax.all_to_all(spread, 'z', 0, 0, axis_index_groups=turned, tiled=True)  22.4 us
    all_to_all x1, blocking collectives, body(): got = lax.all_to_all(send, 'z', 0, 0, axis_index_groups=turned, tiled=True)  15.5 us
    all_to_all x1, blocking collectives, body(): lax.all_to_all(jnp.broadcast_to(got, (n_hi * n_lo,) + got.shape), X, 0, 0...  10.8 us
    all_to_all x1, blocking collectives, body(): lax.all_to_all(send.reshape(n_hi * n_lo, n_z, half, 2 * part), X, 0, 0, t...  9.64 us
    all_to_all x1, blocking collectives, body(): every = lax.all_to_all(copies, 'layer', 0, 0, tiled=True)  8.4 us
    pallas_call x1, Pallas kernels, body(): call(front_kernel, 'front', (jax.ShapeDtypeStruct((tokens, lat), BF16), j...  2.99 us
    pallas_call x1, Pallas kernels, body(): call(decode_kernel, 'decode', (jax.ShapeDtypeStruct(half_sum, F32), jax.S...  2.54 us
    all_gather x1, blocking collectives, body(): got = lax.all_gather(give, 'core', axis=0, tiled=False)  2.18 us

profile of v3, /device:TPU:24, one launch (start us, length us, event | category | flops | bytes accessed | tf_op | source)
XLA Modules:
  0.0 79.5 jit_solution(9297165721034914213)
XLA Ops:
  0.6 0.7 slice_bitcast_fusion.1
  1.3 0.1 pad_add_fusion.place
  1.4 0.1 pad_maximum_fusion
  1.5 22.4 %all_to_all.25 = bf16[16,16,128]{2,1,0:T(8,128)(2,1)S(1)} all-to-all(bf16[16,16,128]{2,1,0:T(8,128)(2,1)S(1)} %broadcast_in_dim.12), channel_id=1, replica_groups={{16,18,20,22,24,26,28,30,0,2,4,6,8,10,12,14},{17,19,21,23,25,27,29,31,1..., dimensions={0} | all-to-all | bytes 131072 | tf_op jit(solution)/shard_map/gather_z/all_to_all | solution.py:189
  23.9 10.8 %all_to_all.26 = bf16[4,16,16,128]{3,2,1,0:T(8,128)(2,1)S(1)} all-to-all(bf16[4,16,16,128]{3,2,1,0:T(8,128)(2,1)S(1)} %broadcast_in_dim.13), channel_id=1, replica_groups=mesh['layer'=4,'x_lo'=2,'core'=2,'z'=16,'x_hi'=2] {'x_hi','x_lo'}, dimensions={0} | all-to-all | bytes 524288 | tf_op jit(solution)/shard_map/gather_x/all_to_all | solution.py:191
  34.7 2.2 %all-gather = bf16[8,16,16,128]{3,2,1,0:T(8,128)(2,1)S(1)} all-gather(bf16[4,16,16,128]{3,2,1,0:T(8,128)(2,1)S(1)} %all_to_all.26), channel_id=2, replica_groups=mesh['layer'=4,'x_lo'=2,'core'=2,'z'=16,'x_hi'=2] {'core'}, dimensions={0}, use_global_device_ids=true | all-gather | bytes 786432 | tf_op jit(solution)/shard_map/gather_core/all_gather | solution.py:193
  36.8 3.0 %front.1 = (bf16[128,128]{1,0:T(8,128)(2,1)}, bf16[4,128,128]{2,1,0:T(8,128)(2,1)S(1)}, f32[128,2048]{1,0:T(8,128)S(1)}) custom-call(s32[2]{0:T(128)S(1)} %pad_add_fusion.place, bf16[2,2,2,16,16,128]{5,4,3,2,1,0:T(8,128)(2,1)S(1)} %bitcast.20, bf16[2048,128]{1,0:T(8,128)(2,1)} %bitcast.25, f32[1,128]{1,0:T(1,128)} %bias.1, bf16[64,2048]{1,0:T(8,128)(2,1)} %bitcast.26, ...), custom_call_target="tpu_custom_call" | custom-call | flops 234881024 | bytes 1835008 | tf_op jit(solution)/shard_map/front/front/pallas_call | solution.py:196
  39.8 8.4 %all_to_all.27.got = bf16[4,128,128]{2,1,0:T(8,128)(2,1)S(1)} all-to-all(bf16[4,128,128]{2,1,0:T(8,128)(2,1)S(1)} %get-tuple-element.11), channel_id=1, replica_groups=mesh['layer'=4,'x_lo'=2,'core'=2,'z'=16,'x_hi'=2] {'layer'}, dimensions={0} | all-to-all | bytes 262144 | tf_op jit(solution)/shard_map/exchange/all_to_all | solution.py:213
  48.2 2.5 %decode.1 = (f32[64,2048]{1,0:T(8,128)S(1)}, bf16[64,2048]{1,0:T(8,128)(2,1)S(1)}) custom-call(s32[2]{0:T(128)S(1)} %pad_add_fusion.place, bf16[4,128,128]{2,1,0:T(8,128)(2,1)S(1)} %all_to_all.27.got, f32[128,2048]{1,0:T(8,128)S(1)} %get-tuple-element.12.partial, bf16[4,128,2048]{2,1,0:T(8,128)(2,1)} %bitcast.24), custom_call_target="tpu_custom_call" | custom-call | flops 201326592 | bytes 1572864 | tf_op jit(solution)/shard_map/decode/decode/pallas_call | solution.py:216
  50.8 2.2 %all-gather.1 = bf16[128,2048]{1,0:T(8,128)(2,1)S(1)} all-gather(bf16[64,2048]{1,0:T(8,128)(2,1)S(1)} %get-tuple-element.14), channel_id=3, replica_groups=mesh['layer'=4,'x_lo'=2,'core'=2,'z'=16,'x_hi'=2] {'core'}, dimensions={0}, use_global_device_ids=true | all-gather | bytes 786432 | tf_op jit(solution)/shard_map/reduce_core/all_gather | solution.py:231
  53.0 0.7 join.1
  53.6 9.6 %all_to_all.28 = bf16[4,16,16,128]{3,2,1,0:T(8,128)(2,1)S(1)} all-to-all(bf16[4,16,16,128]{3,2,1,0:T(8,128)(2,1)S(1)} %bitcast.22), channel_id=1, replica_groups=mesh['layer'=4,'x_lo'=2,'core'=2,'z'=16,'x_hi'=2] {'x_hi','x_lo'}, dimensions={0} | all-to-all | bytes 524288 | tf_op jit(solution)/shard_map/reduce_x/all_to_all | solution.py:242
  63.3 15.5 %all_to_all.29.got = bf16[16,16,128]{2,1,0:T(8,128)(2,1)S(1)} all-to-all(bf16[16,16,128]{2,1,0:T(8,128)(2,1)S(1)} %reduce_sum.12), channel_id=1, replica_groups={{16,18,20,22,24,26,28,30,0,2,4,6,8,10,12,14},{17,19,21,23,25,27,29,31,1..., dimensions={0} | all-to-all | bytes 131072 | tf_op jit(solution)/shard_map/reduce_z/all_to_all | solution.py:245
  78.9 0.7 last.1
  (3 shorter events, 0.1 us)

commit v4 on v2

--- a/solution.py
+++ b/solution.py
@@ -49,6 +49,10 @@
     return lax.broadcasted_iota(jnp.int32, shape, 1) < shape[1] // 2
 
 
+def turn(z, n_z):
+    return (z + n_z // 2) % n_z
+
+
 def start_all(sems, pairs):
     copies = []
     for i, (source, target) in enumerate(pairs):
@@ -62,33 +66,35 @@
         copy.wait()
 
 
-def encode_kernel(got, bias, enc, x, latent, copies, weight, sems):
+def encode_kernel(got, enc, bias, x, own, copies, encs, shift, sems):
     n_core, n_hi, n_lo, n_z, half, lanes = got.shape
-    loads = start_all(sems, [(enc, weight)])
+    loads = start_all(sems, [(enc, encs), (bias, shift)])
     low = low_half((half, lanes))
     for lo in range(n_lo):
         for core in range(n_core):
             row = (lo * n_core + core) * 2 * half
             for z in range(n_z):
-                a = got[core, 0, lo, z].astype(F32)
-                b = got[core, 1, lo, z].astype(F32)
+                at = turn(z, n_z)
+                a = got[core, 0, lo, at].astype(F32)
+                b = got[core, 1, lo, at].astype(F32)
                 top = jnp.where(low, a, pltpu.roll(b, lanes // 2, 1))
                 bottom = jnp.where(low, pltpu.roll(a, lanes // 2, 1), b)
                 cols = slice(z * lanes, (z + 1) * lanes)
                 x[row : row + half, cols] = top.astype(BF16)
                 x[row + half : row + 2 * half, cols] = bottom.astype(BF16)
     wait_all(loads)
-    pre = dot(x[...], weight[...]) + bias[...]
+    pre = dot(x[...], encs[...]) + shift[...]
     value = jnp.maximum(pre, F32(0.0)).astype(BF16)
-    latent[...] = value
+    own[...] = value
     for s in range(copies.shape[0]):
         copies[s] = value
 
 
-def hidden_kernel(layer, x, latent, gate, up, down, dec, out, gates, ups, downs, decs, sems):
+def hidden_kernel(place, x, own, gate, up, down, dec, out, latent, gates, ups, downs, decs, sems):
     loads = start_all(
-        sems, [(gate, gates), (up, ups), (down, downs), (dec.at[layer[0]], decs)]
+        sems, [(gate, gates), (up, ups), (down, downs), (dec.at[place[0]], decs)]
     )
+    latent[...] = own[...]
     rows = x[...]
     wait_all(loads[:2])
     gate_part = dot_t(rows, gates[...])
@@ -97,8 +103,8 @@
     wait_all(loads[2:])
     tile = 256
     for n in range(0, x.shape[1], tile):
-        value = dot(hidden, downs[:, n : n + tile])
-        out[:, n : n + tile] = value - dot(latent[...], decs[:, n : n + tile])
+        cols = slice(n, n + tile)
+        out[:, cols] = dot(hidden, downs[:, cols]) - dot(own[...], decs[:, cols])
 
 
 def decode_kernel(place, got, partial, dec, keep, give, total, decs, sems):
@@ -145,8 +151,9 @@
             cols = slice(z * lanes, (z + 1) * lanes)
             value = keep[row : row + 2 * half, cols] + got[other, row : row + 2 * half, cols].astype(F32)
             top, bottom = value[:half], value[half:]
-            out[0, lo, z] = jnp.where(low, top, pltpu.roll(bottom, lanes // 2, 1)).astype(BF16)
-            out[1, lo, z] = jnp.where(low, pltpu.roll(top, lanes // 2, 1), bottom).astype(BF16)
+            at = turn(z, n_z)
+            out[0, lo, at] = jnp.where(low, top, pltpu.roll(bottom, lanes // 2, 1)).astype(BF16)
+            out[1, lo, at] = jnp.where(low, pltpu.roll(top, lanes // 2, 1), bottom).astype(BF16)
 
 
 def last_kernel(got, out):
@@ -173,14 +180,15 @@
         block = jnp.concatenate([mlp_in[0, :half], mlp_in[0, half:]], axis=1)
         spread = jnp.broadcast_to(block, (n_z, half, 2 * part))
         spread, place = lax.optimization_barrier((spread, place))
-        got = lax.all_to_all(spread, "z", 0, 0, tiled=True)
+        turned = [[turn(z, n_z) for z in range(n_z)]]
+        got = lax.all_to_all(spread, "z", 0, 0, axis_index_groups=turned, tiled=True)
     with jax.named_scope("gather_x"):
         got = lax.all_to_all(jnp.broadcast_to(got, (n_hi * n_lo,) + got.shape), X, 0, 0, tiled=True)
     with jax.named_scope("gather_core"):
         got = lax.all_gather(got, "core", axis=0, tiled=False)
         got = got.reshape(n_core, n_hi, n_lo, n_z, half, 2 * part)
     with jax.named_scope("encode"):
-        x, latent, copies = call(
+        x, own, copies = call(
             encode_kernel,
             "encode",
             (
@@ -188,25 +196,26 @@
                 jax.ShapeDtypeStruct((tokens, lat), BF16),
                 jax.ShapeDtypeStruct((layers, tokens, lat), BF16),
             ),
-            [VMEM, VMEM, ANY],
-            [pltpu.VMEM((width, lat), BF16), dma((1,))],
+            [VMEM, ANY, ANY],
+            [pltpu.VMEM((width, lat), BF16), pltpu.VMEM((1, lat), F32), dma((2,))],
             2 * tokens * width * lat,
             2 * width * lat,
             (VMEM, VMEM, VMEM),
-        )(got, enc_bias, enc)
+        )(got, enc, far(enc_bias))
     with jax.named_scope("exchange"):
         every = lax.all_to_all(copies, "layer", 0, 0, tiled=True)
     with jax.named_scope("hidden"):
-        partial = call(
+        partial, latent = call(
             hidden_kernel,
             "hidden",
-            jax.ShapeDtypeStruct((tokens, width), F32),
+            (jax.ShapeDtypeStruct((tokens, width), F32), jax.ShapeDtypeStruct((tokens, lat), BF16)),
             [SMEM, VMEM, VMEM] + [ANY] * 4,
             [pltpu.VMEM((n_ff, width), BF16) for _ in range(3)]
             + [pltpu.VMEM((lat, width), BF16), dma((4,))],
             6 * tokens * width * n_ff + 2 * tokens * width * lat,
             6 * n_ff * width + 2 * lat * width,
-        )(place, x, latent, gate, up, down, dec)
+            (VMEM, VMEM),
+        )(place, x, own, gate, up, down, dec)
     with jax.named_scope("decode"):
         half_sum = (tokens // n_core, width)
         keep, give = call(
@@ -238,7 +247,7 @@
         got = lax.all_to_all(send.reshape(n_hi * n_lo, n_z, half, 2 * part), X, 0, 0, tiled=True)
         send = got.astype(F32).sum(0).astype(BF16)
     with jax.named_scope("reduce_z"):
-        got = lax.all_to_all(send, "z", 0, 0, tiled=True)
+        got = lax.all_to_all(send, "z", 0, 0, axis_index_groups=turned, tiled=True)
     with jax.named_scope("last"):
         error = call(
             last_kernel,

time: 85.8 us -> 79.5 us (0.927)
  blocking collectives: 68.1 us -> 62.6 us
  local copies, waits for them, and re-layouts: 2.17 us -> 0.75 us
    all_to_all x2, blocking collectives: 43.4 us -> 37.9 us  [the longest x1 22.4 us: body(): lax.all_to_all(spread, 'z', 0, 0, axis_index_groups=turned, tiled=True)]
    unnamed x4 -> x0, local copies, waits for them, and re-layouts: 1.41 us -> none
  transfers between devices with their start and end apart: 1 -> 1, of which waited for: 1 -> 1; matrix products, arithmetic and copies ran while one was open for 0% -> 0% of each run, Pallas kernels for 3% -> 4%
where the time goes in v4:
time: 79.5 us; the launch traced here: 78.8 us
  blocking collectives  62.6 us (79%)
  Pallas kernels  8.87 us (11%)
  starting transfers between devices  4.7 us (6%)
  waiting for transfers between devices  0.96 us (1%)
    all_to_all x1, blocking collectives, body(): lax.all_to_all(spread, 'z', 0, 0, axis_index_groups=turned, tiled=True)  22.4 us
    all_to_all x1, blocking collectives, body(): got = lax.all_to_all(send, 'z', 0, 0, axis_index_groups=turned, tiled=True)  15.5 us
    all_to_all x1, blocking collectives, body(): lax.all_to_all(jnp.broadcast_to(got, (n_hi * n_lo,) + got.shape), X, 0, 0...  10.8 us
    all_to_all x1, blocking collectives, body(): lax.all_to_all(send.reshape(n_hi * n_lo, n_z, half, 2 * part), X, 0, 0, t...  9.64 us
    all_to_all x1, starting transfers between devices, body(): every = lax.all_to_all(copies, 'layer', 0, 0, tiled=True)  4.7 us
    pallas_call x1, Pallas kernels, body(): call(hidden_kernel, 'hidden', (jax.ShapeDtypeStruct((tokens, width), F32)...  2.95 us
    pallas_call x1, Pallas kernels, body(): call(decode_kernel, 'decode', (jax.ShapeDtypeStruct(half_sum, F32), jax.S...  2.54 us
    all_gather x1, blocking collectives, body(): got = lax.all_gather(give, 'core', axis=0, tiled=False)  2.18 us
  transfers between devices with their start and end apart: 1, of which 1 were waited for; matrix products, arithmetic and copies ran while one was open for 0% of the time, Pallas kernels for 4%

profile of v4, /device:TPU:24, one launch (start us, length us, event | category | flops | bytes accessed | tf_op | source)
XLA Modules:
  0.0 78.8 jit_solution(7141689244640880833)
XLA Ops:
  0.6 0.7 slice_bitcast_fusion.1
  1.3 0.1 pad_add_fusion.place
  1.4 0.1 pad_maximum_fusion
  1.5 22.4 %all_to_all.25 = bf16[16,16,128]{2,1,0:T(8,128)(2,1)S(1)} all-to-all(bf16[16,16,128]{2,1,0:T(8,128)(2,1)S(1)} %broadcast_in_dim.12), channel_id=1, replica_groups={{16,18,20,22,24,26,28,30,0,2,4,6,8,10,12,14},{17,19,21,23,25,27,29,31,1..., dimensions={0} | all-to-all | bytes 131072 | tf_op jit(solution)/shard_map/gather_z/all_to_all | solution.py:184
  23.9 10.8 %all_to_all.26 = bf16[4,16,16,128]{3,2,1,0:T(8,128)(2,1)S(1)} all-to-all(bf16[4,16,16,128]{3,2,1,0:T(8,128)(2,1)S(1)} %broadcast_in_dim.13), channel_id=1, replica_groups=mesh['layer'=4,'x_lo'=2,'core'=2,'z'=16,'x_hi'=2] {'x_hi','x_lo'}, dimensions={0} | all-to-all | bytes 524288 | tf_op jit(solution)/shard_map/gather_x/all_to_all | solution.py:186
  34.7 2.2 %all-gather = bf16[8,16,16,128]{3,2,1,0:T(8,128)(2,1)S(1)} all-gather(bf16[4,16,16,128]{3,2,1,0:T(8,128)(2,1)S(1)} %all_to_all.26), channel_id=2, replica_groups=mesh['layer'=4,'x_lo'=2,'core'=2,'z'=16,'x_hi'=2] {'core'}, dimensions={0}, use_global_device_ids=true | all-gather | bytes 786432 | tf_op jit(solution)/shard_map/gather_core/all_gather | solution.py:188
  36.8 2.0 %encode.1 = (bf16[128,2048]{1,0:T(8,128)(2,1)S(1)}, bf16[128,128]{1,0:T(8,128)(2,1)S(1)}, bf16[4,128,128]{2,1,0:T(8,128)(2,1)}) custom-call(bf16[2,2,2,16,16,128]{5,4,3,2,1,0:T(8,128)(2,1)S(1)} %bitcast.21, bf16[2048,128]{1,0:T(8,128)(2,1)} %bitcast.25, f32[1,128]{1,0:T(1,128)} %bias.1), custom_call_target="tpu_custom_call" | custom-call | flops 67108864 | bytes 524288 | tf_op jit(solution)/shard_map/encode/encode/pallas_call | solution.py:191
  38.9 4.7 %all-to-all-start.2 = ((bf16[4,128,128]{2,1,0:T(8,128)(2,1)}), bf16[4,128,128]{2,1,0:T(8,128)(2,1)S(1)}, u32[]{:S(2)}, u32[]{:S(2)}) async-start(bf16[4,128,128]{2,1,0:T(8,128)(2,1)} %get-tuple-element.13), calls=%async_computation.2 | async-start | bytes 262144 | tf_op jit(solution)/shard_map/exchange/all_to_all | solution.py:206
  43.6 2.9 %hidden.1 = (f32[128,2048]{1,0:T(8,128)S(1)}, bf16[128,128]{1,0:T(8,128)(2,1)}) custom-call(s32[2]{0:T(128)S(1)} %pad_add_fusion.place, bf16[128,2048]{1,0:T(8,128)(2,1)S(1)} %get-tuple-element.14.x, bf16[128,128]{1,0:T(8,128)(2,1)S(1)} %get-tuple-element.15.own, bf16[64,2048]{1,0:T(8,128)(2,1)} %bitcast.26, bf16[64,2048]{1,0:T(8,128)(2,1)} %bitcast.27, ...), custom_call_target="tpu_custom_call" | custom-call | flops 167772160 | bytes 1310720 | tf_op jit(solution)/shard_map/hidden/hidden/pallas_call | solution.py:208
  46.5 1.0 %all-to-all-done.2.got = bf16[4,128,128]{2,1,0:T(8,128)(2,1)S(1)} async-done(((bf16[4,128,128]{2,1,0:T(8,128)(2,1)}), bf16[4,128,128]{2,1,0:T(8,128)(2,1)S(1)}, u32[]{:S(2)}, u32[]{:S(2)}) %all-to-all-start.2) | async-done | bytes 131104 | tf_op jit(solution)/shard_map/exchange/all_to_all | solution.py:206
  47.5 2.5 %decode.1 = (f32[64,2048]{1,0:T(8,128)S(1)}, bf16[64,2048]{1,0:T(8,128)(2,1)S(1)}) custom-call(s32[2]{0:T(128)S(1)} %pad_add_fusion.place, bf16[4,128,128]{2,1,0:T(8,128)(2,1)S(1)} %all-to-all-done.2.got, f32[128,2048]{1,0:T(8,128)S(1)} %get-tuple-element.16.partial, bf16[4,128,2048]{2,1,0:T(8,128)(2,1)} %bitcast.24), custom_call_target="tpu_custom_call" | custom-call | flops 201326592 | bytes 1572864 | tf_op jit(solution)/shard_map/decode/decode/pallas_call | solution.py:221
  50.0 2.2 %all-gather.1 = bf16[128,2048]{1,0:T(8,128)(2,1)S(1)} all-gather(bf16[64,2048]{1,0:T(8,128)(2,1)S(1)} %get-tuple-element.18), channel_id=3, replica_groups=mesh['layer'=4,'x_lo'=2,'core'=2,'z'=16,'x_hi'=2] {'core'}, dimensions={0}, use_global_device_ids=true | all-gather | bytes 786432 | tf_op jit(solution)/shard_map/reduce_core/all_gather | solution.py:236
  52.2 0.7 join.1
  52.9 9.6 %all_to_all.27 = bf16[4,16,16,128]{3,2,1,0:T(8,128)(2,1)S(1)} all-to-all(bf16[4,16,16,128]{3,2,1,0:T(8,128)(2,1)S(1)} %bitcast.22), channel_id=1, replica_groups=mesh['layer'=4,'x_lo'=2,'core'=2,'z'=16,'x_hi'=2] {'x_hi','x_lo'}, dimensions={0} | all-to-all | bytes 524288 | tf_op jit(solution)/shard_map/reduce_x/all_to_all | solution.py:247
  62.6 15.5 %all_to_all.28.got = bf16[16,16,128]{2,1,0:T(8,128)(2,1)S(1)} all-to-all(bf16[16,16,128]{2,1,0:T(8,128)(2,1)S(1)} %reduce_sum.12), channel_id=1, replica_groups={{16,18,20,22,24,26,28,30,0,2,4,6,8,10,12,14},{17,19,21,23,25,27,29,31,1..., dimensions={0} | all-to-all | bytes 131072 | tf_op jit(solution)/shard_map/reduce_z/all_to_all | solution.py:250
  78.1 0.7 last.1
  (3 shorter events, 0.1 us)
Async XLA Ops:
  38.9 8.6 %all-to-all-start.2 = ((bf16[4,128,128]{2,1,0:T(8,128)(2,1)}), bf16[4,128,128]{2,1,0:T(8,128)(2,1)S(1)}, u32[]{:S(2)}, u32[]{:S(2)}) async-start(bf16[4,128,128]{2,1,0:T(8,128)(2,1)} %get-tuple-element.13), calls=%async_computation.2 | async-start | bytes 262144 | tf_op jit(solution)/shard_map/exchange/all_to_all | solution.py:206

commit v5 on v4

--- a/solution.py
+++ b/solution.py
@@ -66,9 +66,9 @@
         copy.wait()
 
 
-def encode_kernel(got, enc, bias, x, own, copies, encs, shift, sems):
+def encode_kernel(got, enc, bias, x, own, copies, shift, sems):
     n_core, n_hi, n_lo, n_z, half, lanes = got.shape
-    loads = start_all(sems, [(enc, encs), (bias, shift)])
+    loads = start_all(sems, [(bias, shift)])
     low = low_half((half, lanes))
     for lo in range(n_lo):
         for core in range(n_core):
@@ -83,7 +83,7 @@
                 x[row : row + half, cols] = top.astype(BF16)
                 x[row + half : row + 2 * half, cols] = bottom.astype(BF16)
     wait_all(loads)
-    pre = dot(x[...], encs[...]) + shift[...]
+    pre = dot(x[...], enc[...]) + shift[...]
     value = jnp.maximum(pre, F32(0.0)).astype(BF16)
     own[...] = value
     for s in range(copies.shape[0]):
@@ -172,7 +172,8 @@
     rows, part = mlp_in.shape[1:]
     half, tokens = rows // 2, rows * n_lo * n_core
     gate, up, down = far(gate_weight[0].T), far(up_weight[0].T), far(down_weight[0])
-    enc, dec = far(enc_weight[0]), far(dec_weight[0])
+    enc = pltpu.with_memory_space_constraint(enc_weight[0], pltpu.VMEM)
+    dec = far(dec_weight[0])
     width, lat = enc.shape
     n_ff = gate.shape[0]
     dma = pltpu.SemaphoreType.DMA
@@ -196,8 +197,8 @@
                 jax.ShapeDtypeStruct((tokens, lat), BF16),
                 jax.ShapeDtypeStruct((layers, tokens, lat), BF16),
             ),
-            [VMEM, ANY, ANY],
-            [pltpu.VMEM((width, lat), BF16), pltpu.VMEM((1, lat), F32), dma((2,))],
+            [VMEM, VMEM, ANY],
+            [pltpu.VMEM((1, lat), F32), dma((1,))],
             2 * tokens * width * lat,
             2 * width * lat,
             (VMEM, VMEM, VMEM),

time: 79.5 us -> 79.2 us (level)
  no operation moved by 1% of the time
where the time goes in v5:
time: 79.2 us; the launch traced here: 78.5 us
  blocking collectives  62.6 us (79%)
  Pallas kernels  8.47 us (11%)
  starting transfers between devices  4.7 us (6%)
  waiting for transfers between devices  0.96 us (1%)
  local copies, waits for them, and re-layouts  0.81 us (1%)
    all_to_all x1, blocking collectives, body(): lax.all_to_all(spread, 'z', 0, 0, axis_index_groups=turned, tiled=True)  22.4 us
    all_to_all x1, blocking collectives, body(): got = lax.all_to_all(send, 'z', 0, 0, axis_index_groups=turned, tiled=True)  15.5 us
    all_to_all x1, blocking collectives, body(): lax.all_to_all(jnp.broadcast_to(got, (n_hi * n_lo,) + got.shape), X, 0, 0...  10.8 us
    all_to_all x1, blocking collectives, body(): lax.all_to_all(send.reshape(n_hi * n_lo, n_z, half, 2 * part), X, 0, 0, t...  9.64 us
    all_to_all x1, starting transfers between devices, body(): every = lax.all_to_all(copies, 'layer', 0, 0, tiled=True)  4.7 us
    pallas_call x1, Pallas kernels, body(): call(hidden_kernel, 'hidden', (jax.ShapeDtypeStruct((tokens, width), F32)...  2.94 us
    pallas_call x1, Pallas kernels, body(): call(decode_kernel, 'decode', (jax.ShapeDtypeStruct(half_sum, F32), jax.S...  2.54 us
    all_gather x1, blocking collectives, body(): got = lax.all_gather(give, 'core', axis=0, tiled=False)  2.18 us
  transfers between devices with their start and end apart: 1, of which 1 were waited for; matrix products, arithmetic and copies ran while one was open for 0% of the time, Pallas kernels for 4%

profile of v5, /device:TPU:24, one launch (start us, length us, event | category | flops | bytes accessed | tf_op | source)
XLA Modules:
  0.0 78.5 jit_solution(12251223589488541770)
XLA Ops:
  0.6 0.0 copy-start
  0.6 0.8 slice_bitcast_fusion.1
  1.4 0.1 pad_add_fusion.place
  1.5 0.1 pad_maximum_fusion
  1.6 22.4 %all_to_all.25 = bf16[16,16,128]{2,1,0:T(8,128)(2,1)S(1)} all-to-all(bf16[16,16,128]{2,1,0:T(8,128)(2,1)S(1)} %broadcast_in_dim.12), channel_id=1, replica_groups={{16,18,20,22,24,26,28,30,0,2,4,6,8,10,12,14},{17,19,21,23,25,27,29,31,1..., dimensions={0} | all-to-all | bytes 131072 | tf_op jit(solution)/shard_map/gather_z/all_to_all | solution.py:185
  24.0 10.8 %all_to_all.26 = bf16[4,16,16,128]{3,2,1,0:T(8,128)(2,1)S(1)} all-to-all(bf16[4,16,16,128]{3,2,1,0:T(8,128)(2,1)S(1)} %broadcast_in_dim.13), channel_id=1, replica_groups=mesh['layer'=4,'x_lo'=2,'core'=2,'z'=16,'x_hi'=2] {'x_hi','x_lo'}, dimensions={0} | all-to-all | bytes 524288 | tf_op jit(solution)/shard_map/gather_x/all_to_all | solution.py:187
  34.7 2.2 %all-gather = bf16[8,16,16,128]{3,2,1,0:T(8,128)(2,1)S(1)} all-gather(bf16[4,16,16,128]{3,2,1,0:T(8,128)(2,1)S(1)} %all_to_all.26), channel_id=2, replica_groups=mesh['layer'=4,'x_lo'=2,'core'=2,'z'=16,'x_hi'=2] {'core'}, dimensions={0}, use_global_device_ids=true | all-gather | bytes 786432 | tf_op jit(solution)/shard_map/gather_core/all_gather | solution.py:189
  36.9 0.0 copy-done
  36.9 1.6 %encode.1 = (bf16[128,2048]{1,0:T(8,128)(2,1)S(1)}, bf16[128,128]{1,0:T(8,128)(2,1)S(1)}, bf16[4,128,128]{2,1,0:T(8,128)(2,1)}) custom-call(bf16[2,2,2,16,16,128]{5,4,3,2,1,0:T(8,128)(2,1)S(1)} %bitcast.21, bf16[2048,128]{1,0:T(8,128)(2,1)S(1)} %bitcast.23, f32[1,128]{1,0:T(1,128)} %bias.1), custom_call_target="tpu_custom_call" | custom-call | flops 67108864 | bytes 524288 | tf_op jit(solution)/shard_map/encode/encode/pallas_call | solution.py:192
  38.5 4.7 %all-to-all-start.2 = ((bf16[4,128,128]{2,1,0:T(8,128)(2,1)}), bf16[4,128,128]{2,1,0:T(8,128)(2,1)S(1)}, u32[]{:S(2)}, u32[]{:S(2)}) async-start(bf16[4,128,128]{2,1,0:T(8,128)(2,1)} %get-tuple-element.13), calls=%async_computation.2 | async-start | bytes 262144 | tf_op jit(solution)/shard_map/exchange/all_to_all | solution.py:207
  43.2 2.9 %hidden.1 = (f32[128,2048]{1,0:T(8,128)S(1)}, bf16[128,128]{1,0:T(8,128)(2,1)}) custom-call(s32[2]{0:T(128)S(1)} %pad_add_fusion.place, bf16[128,2048]{1,0:T(8,128)(2,1)S(1)} %get-tuple-element.14.x, bf16[128,128]{1,0:T(8,128)(2,1)S(1)} %get-tuple-element.15.own, bf16[64,2048]{1,0:T(8,128)(2,1)} %bitcast.26, bf16[64,2048]{1,0:T(8,128)(2,1)} %bitcast.27, ...), custom_call_target="tpu_custom_call" | custom-call | flops 167772160 | bytes 1310720 | tf_op jit(solution)/shard_map/hidden/hidden/pallas_call | solution.py:209
  46.2 1.0 %all-to-all-done.2.got = bf16[4,128,128]{2,1,0:T(8,128)(2,1)S(1)} async-done(((bf16[4,128,128]{2,1,0:T(8,128)(2,1)}), bf16[4,128,128]{2,1,0:T(8,128)(2,1)S(1)}, u32[]{:S(2)}, u32[]{:S(2)}) %all-to-all-start.2) | async-done | bytes 131104 | tf_op jit(solution)/shard_map/exchange/all_to_all | solution.py:207
  47.1 2.5 %decode.1 = (f32[64,2048]{1,0:T(8,128)S(1)}, bf16[64,2048]{1,0:T(8,128)(2,1)S(1)}) custom-call(s32[2]{0:T(128)S(1)} %pad_add_fusion.place, bf16[4,128,128]{2,1,0:T(8,128)(2,1)S(1)} %all-to-all-done.2.got, f32[128,2048]{1,0:T(8,128)S(1)} %get-tuple-element.16.partial, bf16[4,128,2048]{2,1,0:T(8,128)(2,1)} %bitcast.25), custom_call_target="tpu_custom_call" | custom-call | flops 201326592 | bytes 1572864 | tf_op jit(solution)/shard_map/decode/decode/pallas_call | solution.py:222
  49.7 2.2 %all-gather.1 = bf16[128,2048]{1,0:T(8,128)(2,1)S(1)} all-gather(bf16[64,2048]{1,0:T(8,128)(2,1)S(1)} %get-tuple-element.18), channel_id=3, replica_groups=mesh['layer'=4,'x_lo'=2,'core'=2,'z'=16,'x_hi'=2] {'core'}, dimensions={0}, use_global_device_ids=true | all-gather | bytes 786432 | tf_op jit(solution)/shard_map/reduce_core/all_gather | solution.py:237
  51.9 0.7 join.1
  52.6 9.6 %all_to_all.27 = bf16[4,16,16,128]{3,2,1,0:T(8,128)(2,1)S(1)} all-to-all(bf16[4,16,16,128]{3,2,1,0:T(8,128)(2,1)S(1)} %bitcast.22), channel_id=1, replica_groups=mesh['layer'=4,'x_lo'=2,'core'=2,'z'=16,'x_hi'=2] {'x_hi','x_lo'}, dimensions={0} | all-to-all | bytes 524288 | tf_op jit(solution)/shard_map/reduce_x/all_to_all | solution.py:248
  62.2 15.5 %all_to_all.28.got = bf16[16,16,128]{2,1,0:T(8,128)(2,1)S(1)} all-to-all(bf16[16,16,128]{2,1,0:T(8,128)(2,1)S(1)} %reduce_sum.12), channel_id=1, replica_groups={{16,18,20,22,24,26,28,30,0,2,4,6,8,10,12,14},{17,19,21,23,25,27,29,31,1..., dimensions={0} | all-to-all | bytes 131072 | tf_op jit(solution)/shard_map/reduce_z/all_to_all | solution.py:251
  77.8 0.7 last.1
  (3 shorter events, 0.1 us)
Async XLA Ops:
  0.6 36.3 %copy-start = (bf16[1,2048,128]{2,1,0:T(8,128)(2,1)S(1)}, bf16[1,2048,128]{2,1,0:T(8,128)(2,1)}, u32[]{:S(2)}) copy-start(bf16[1,2048,128]{2,1,0:T(8,128)(2,1)} %param.11) | copy-start | bytes 1572868
  38.5 8.6 %all-to-all-start.2 = ((bf16[4,128,128]{2,1,0:T(8,128)(2,1)}), bf16[4,128,128]{2,1,0:T(8,128)(2,1)S(1)}, u32[]{:S(2)}, u32[]{:S(2)}) async-start(bf16[4,128,128]{2,1,0:T(8,128)(2,1)} %get-tuple-element.13), calls=%async_computation.2 | async-start | bytes 262144 | tf_op jit(solution)/shard_map/exchange/all_to_all | solution.py:207

commit v6 on v5

--- a/solution.py
+++ b/solution.py
@@ -67,7 +67,7 @@
 
 
 def encode_kernel(got, enc, bias, x, own, copies, shift, sems):
-    n_core, n_hi, n_lo, n_z, half, lanes = got.shape
+    n_lo, n_core, n_z, n_hi, half, lanes = got.shape
     loads = start_all(sems, [(bias, shift)])
     low = low_half((half, lanes))
     for lo in range(n_lo):
@@ -75,8 +75,8 @@
             row = (lo * n_core + core) * 2 * half
             for z in range(n_z):
                 at = turn(z, n_z)
-                a = got[core, 0, lo, at].astype(F32)
-                b = got[core, 1, lo, at].astype(F32)
+                a = got[lo, core, at, 0].astype(F32)
+                b = got[lo, core, at, 1].astype(F32)
                 top = jnp.where(low, a, pltpu.roll(b, lanes // 2, 1))
                 bottom = jnp.where(low, pltpu.roll(a, lanes // 2, 1), b)
                 cols = slice(z * lanes, (z + 1) * lanes)
@@ -177,17 +177,16 @@
     width, lat = enc.shape
     n_ff = gate.shape[0]
     dma = pltpu.SemaphoreType.DMA
-    with jax.named_scope("gather_z"):
+    turned = [[turn(z, n_z) for z in range(n_z)]]
+    with jax.named_scope("gather_mp"):
         block = jnp.concatenate([mlp_in[0, :half], mlp_in[0, half:]], axis=1)
-        spread = jnp.broadcast_to(block, (n_z, half, 2 * part))
+        spread = jnp.broadcast_to(block, (n_z * n_hi, half, 2 * part))
         spread, place = lax.optimization_barrier((spread, place))
-        turned = [[turn(z, n_z) for z in range(n_z)]]
-        got = lax.all_to_all(spread, "z", 0, 0, axis_index_groups=turned, tiled=True)
-    with jax.named_scope("gather_x"):
-        got = lax.all_to_all(jnp.broadcast_to(got, (n_hi * n_lo,) + got.shape), X, 0, 0, tiled=True)
-    with jax.named_scope("gather_core"):
-        got = lax.all_gather(got, "core", axis=0, tiled=False)
-        got = got.reshape(n_core, n_hi, n_lo, n_z, half, 2 * part)
+        pairs = [[turn(z, n_z) * n_hi + hi for z in range(n_z) for hi in range(n_hi)]]
+        got = lax.all_to_all(spread, MP, 0, 0, axis_index_groups=pairs, tiled=True)
+    with jax.named_scope("gather_dp"):
+        got = lax.all_gather(got, DP, axis=0, tiled=False)
+        got = got.reshape(n_lo, n_core, n_z, n_hi, half, 2 * part)
     with jax.named_scope("encode"):
         x, own, copies = call(
             encode_kernel,

time: 79.2 us -> 81.5 us (1.029)
  blocking collectives: 62.6 us -> 64 us
  local copies, waits for them, and re-layouts: 0.81 us -> 1.77 us
    all_gather x1, blocking collectives: 2.17 us -> 6.49 us  [body(): got = lax.all_gather(got, DP, axis=0, tiled=False)]
    all_to_all x2 -> x1, blocking collectives: 33.1 us -> 30.1 us  [body(): got = lax.all_to_all(spread, MP, 0, 0, axis_index_groups=pairs, tiled=True)]
    unnamed x2, local copies, waits for them, and re-layouts: 0.01 us -> 1.04 us
where the time goes in v6:
time: 81.5 us; the launch traced here: 80.8 us
  blocking collectives  64 us (79%)
  Pallas kernels  8.46 us (10%)
  starting transfers between devices  4.7 us (6%)
  local copies, waits for them, and re-layouts  1.77 us (2%)
  waiting for transfers between devices  0.96 us (1%)
    all_to_all x1, blocking collectives, body(): got = lax.all_to_all(spread, MP, 0, 0, axis_index_groups=pairs, tiled=True)  30.1 us
    all_to_all x1, blocking collectives, body(): got = lax.all_to_all(send, 'z', 0, 0, axis_index_groups=turned, tiled=True)  15.6 us
    all_to_all x1, blocking collectives, body(): lax.all_to_all(send.reshape(n_hi * n_lo, n_z, half, 2 * part), X, 0, 0, t...  9.64 us
    all_gather x1, blocking collectives, body(): got = lax.all_gather(got, DP, axis=0, tiled=False)  6.49 us
    all_to_all x1, starting transfers between devices, body(): every = lax.all_to_all(copies, 'layer', 0, 0, tiled=True)  4.7 us
    pallas_call x1, Pallas kernels, body(): call(hidden_kernel, 'hidden', (jax.ShapeDtypeStruct((tokens, width), F32)...  2.94 us
    pallas_call x1, Pallas kernels, body(): call(decode_kernel, 'decode', (jax.ShapeDtypeStruct(half_sum, F32), jax.S...  2.53 us
    all_gather x1, blocking collectives, body(): got = lax.all_gather(give, 'core', axis=0, tiled=False)  2.18 us
  transfers between devices with their start and end apart: 1, of which 1 were waited for; matrix products, arithmetic and copies ran while one was open for 0% of the time, Pallas kernels for 4%

profile of v6, /device:TPU:24, one launch (start us, length us, event | category | flops | bytes accessed | tf_op | source)
XLA Modules:
  0.0 80.8 jit_solution(10216399069515408005)
XLA Ops:
  0.6 0.7 slice_bitcast_fusion.1
  1.3 0.1 pad_add_fusion.place
  1.4 0.1 pad_maximum_fusion
  1.5 30.1 %all_to_all.20 = bf16[32,16,128]{2,1,0:T(8,128)(2,1)S(1)} all-to-all(bf16[32,16,128]{2,1,0:T(8,128)(2,1)S(1)} %broadcast_in_dim.9), channel_id=1, replica_groups={{16,17,18,19,20,21,22,23,24,25,26,27,28,29,30,31,0,1,2,3,4,5,6,7,8,9,10..., dimensions={0} | all-to-all | bytes 262144 | tf_op jit(solution)/shard_map/gather_mp/all_to_all | solution.py:186
  31.6 6.5 %all-gather = bf16[128,16,128]{2,1,0:T(8,128)(2,1)S(1)} all-gather(bf16[32,16,128]{2,1,0:T(8,128)(2,1)S(1)} %all_to_all.20), channel_id=2, replica_groups=mesh['layer'=4,'x_lo'=2,'core'=2,'z'=16,'x_hi'=2] {'x_lo','core'}, dimensions={0}, use_global_device_ids=true | all-gather | bytes 655360 | tf_op jit(solution)/shard_map/gather_dp/all_gather | solution.py:188
  38.1 0.0 copy-start
  38.1 1.0 %copy-done = bf16[1,2048,128]{2,1,0:T(8,128)(2,1)S(1)} copy-done((bf16[1,2048,128]{2,1,0:T(8,128)(2,1)S(1)}, bf16[1,2048,128]{2,1,0:T(8,128)(2,1)}, u32[]{:S(2)}) %copy-start) | copy-done | bytes 524312
  39.1 1.6 %encode.1 = (bf16[128,2048]{1,0:T(8,128)(2,1)S(1)}, bf16[128,128]{1,0:T(8,128)(2,1)S(1)}, bf16[4,128,128]{2,1,0:T(8,128)(2,1)}) custom-call(bf16[2,2,16,2,16,128]{5,4,3,2,1,0:T(8,128)(2,1)S(1)} %bitcast.21, bf16[2048,128]{1,0:T(8,128)(2,1)S(1)} %bitcast.23, f32[1,128]{1,0:T(1,128)} %bias.1), custom_call_target="tpu_custom_call" | custom-call | flops 67108864 | bytes 524288 | tf_op jit(solution)/shard_map/encode/encode/pallas_call | solution.py:191
  40.7 4.7 %all-to-all-start.1 = ((bf16[4,128,128]{2,1,0:T(8,128)(2,1)}), bf16[4,128,128]{2,1,0:T(8,128)(2,1)S(1)}, u32[]{:S(2)}, u32[]{:S(2)}) async-start(bf16[4,128,128]{2,1,0:T(8,128)(2,1)} %get-tuple-element.13), calls=%async_computation.1 | async-start | bytes 262144 | tf_op jit(solution)/shard_map/exchange/all_to_all | solution.py:206
  45.4 2.9 %hidden.1 = (f32[128,2048]{1,0:T(8,128)S(1)}, bf16[128,128]{1,0:T(8,128)(2,1)}) custom-call(s32[2]{0:T(128)S(1)} %pad_add_fusion.place, bf16[128,2048]{1,0:T(8,128)(2,1)S(1)} %get-tuple-element.14.x, bf16[128,128]{1,0:T(8,128)(2,1)S(1)} %get-tuple-element.15.own, bf16[64,2048]{1,0:T(8,128)(2,1)} %bitcast.26, bf16[64,2048]{1,0:T(8,128)(2,1)} %bitcast.27, ...), custom_call_target="tpu_custom_call" | custom-call | flops 167772160 | bytes 1310720 | tf_op jit(solution)/shard_map/hidden/hidden/pallas_call | solution.py:208
  48.4 1.0 %all-to-all-done.1.got = bf16[4,128,128]{2,1,0:T(8,128)(2,1)S(1)} async-done(((bf16[4,128,128]{2,1,0:T(8,128)(2,1)}), bf16[4,128,128]{2,1,0:T(8,128)(2,1)S(1)}, u32[]{:S(2)}, u32[]{:S(2)}) %all-to-all-start.1) | async-done | bytes 131104 | tf_op jit(solution)/shard_map/exchange/all_to_all | solution.py:206
  49.3 2.5 %decode.1 = (f32[64,2048]{1,0:T(8,128)S(1)}, bf16[64,2048]{1,0:T(8,128)(2,1)S(1)}) custom-call(s32[2]{0:T(128)S(1)} %pad_add_fusion.place, bf16[4,128,128]{2,1,0:T(8,128)(2,1)S(1)} %all-to-all-done.1.got, f32[128,2048]{1,0:T(8,128)S(1)} %get-tuple-element.16.partial, bf16[4,128,2048]{2,1,0:T(8,128)(2,1)} %bitcast.25), custom_call_target="tpu_custom_call" | custom-call | flops 201326592 | bytes 1572864 | tf_op jit(solution)/shard_map/decode/decode/pallas_call | solution.py:221
  51.9 2.2 %all-gather.1 = bf16[128,2048]{1,0:T(8,128)(2,1)S(1)} all-gather(bf16[64,2048]{1,0:T(8,128)(2,1)S(1)} %get-tuple-element.18), channel_id=3, replica_groups=mesh['layer'=4,'x_lo'=2,'core'=2,'z'=16,'x_hi'=2] {'core'}, dimensions={0}, use_global_device_ids=true | all-gather | bytes 786432 | tf_op jit(solution)/shard_map/reduce_core/all_gather | solution.py:236
  54.1 0.7 join.1
  54.8 9.6 %all_to_all.21 = bf16[4,16,16,128]{3,2,1,0:T(8,128)(2,1)S(1)} all-to-all(bf16[4,16,16,128]{3,2,1,0:T(8,128)(2,1)S(1)} %bitcast.22), channel_id=1, replica_groups=mesh['layer'=4,'x_lo'=2,'core'=2,'z'=16,'x_hi'=2] {'x_hi','x_lo'}, dimensions={0} | all-to-all | bytes 524288 | tf_op jit(solution)/shard_map/reduce_x/all_to_all | solution.py:247
  64.4 15.6 %all_to_all.22.got = bf16[16,16,128]{2,1,0:T(8,128)(2,1)S(1)} all-to-all(bf16[16,16,128]{2,1,0:T(8,128)(2,1)S(1)} %reduce_sum.12), channel_id=1, replica_groups={{16,18,20,22,24,26,28,30,0,2,4,6,8,10,12,14},{17,19,21,23,25,27,29,31,1..., dimensions={0} | all-to-all | bytes 131072 | tf_op jit(solution)/shard_map/reduce_z/all_to_all | solution.py:250
  80.1 0.7 last.1
  (2 shorter events, 0.1 us)
Async XLA Ops:
  38.1 1.0 %copy-start = (bf16[1,2048,128]{2,1,0:T(8,128)(2,1)S(1)}, bf16[1,2048,128]{2,1,0:T(8,128)(2,1)}, u32[]{:S(2)}) copy-start(bf16[1,2048,128]{2,1,0:T(8,128)(2,1)} %param.11) | copy-start | bytes 1572868
  40.7 8.6 %all-to-all-start.1 = ((bf16[4,128,128]{2,1,0:T(8,128)(2,1)}), bf16[4,128,128]{2,1,0:T(8,128)(2,1)S(1)}, u32[]{:S(2)}, u32[]{:S(2)}) async-start(bf16[4,128,128]{2,1,0:T(8,128)(2,1)} %get-tuple-element.13), calls=%async_computation.1 | async-start | bytes 262144 | tf_op jit(solution)/shard_map/exchange/all_to_all | solution.py:206

commit v7 on v5

--- a/solution.py
+++ b/solution.py
@@ -12,7 +12,6 @@
 BF16 = jnp.bfloat16
 VMEM_BYTES = 8 * 2**20
 VMEM = pl.BlockSpec(memory_space=pltpu.VMEM)
-SMEM = pl.BlockSpec(memory_space=pltpu.SMEM)
 ANY = pl.BlockSpec(memory_space=pl.ANY)
 
 
@@ -90,9 +89,9 @@
         copies[s] = value
 
 
-def hidden_kernel(place, x, own, gate, up, down, dec, out, latent, gates, ups, downs, decs, sems):
+def hidden_kernel(x, own, gate, up, down, dec, out, latent, gates, ups, downs, decs, sems):
     loads = start_all(
-        sems, [(gate, gates), (up, ups), (down, downs), (dec.at[place[0]], decs)]
+        sems, [(gate, gates), (up, ups), (down, downs), (dec.at[lax.axis_index("layer")], decs)]
     )
     latent[...] = own[...]
     rows = x[...]
@@ -107,9 +106,9 @@
         out[:, cols] = dot(hidden, downs[:, cols]) - dot(own[...], decs[:, cols])
 
 
-def decode_kernel(place, got, partial, dec, keep, give, total, decs, sems):
+def decode_kernel(got, partial, dec, keep, give, total, decs, sems):
     n_src = got.shape[0]
-    layer, core = place[0], place[1]
+    layer, core = lax.axis_index("layer"), lax.axis_index("core")
 
     def load(back):
         return pltpu.make_async_copy(dec.at[layer - back], decs.at[back - 1], sems.at[back - 1])
@@ -141,9 +140,9 @@
         give[lo * rows : (lo + 1) * rows] = total[pl.ds(theirs, rows)].astype(BF16)
 
 
-def join_kernel(place, keep, got, out):
+def join_kernel(keep, got, out):
     n_hi, n_lo, n_z, half, lanes = out.shape
-    other = 1 - place[1]
+    other = 1 - lax.axis_index("core")
     low = low_half((half, lanes))
     for lo in range(n_lo):
         row = lo * 2 * half
@@ -166,7 +165,6 @@
 
 
 def body(mlp_in, gate_weight, up_weight, down_weight, enc_weight, enc_bias, dec_weight):
-    place = jnp.stack([lax.axis_index("layer"), lax.axis_index("core")]).astype(jnp.int32)
     layers, n_core = lax.axis_size("layer"), lax.axis_size("core")
     n_z, n_hi, n_lo = lax.axis_size("z"), lax.axis_size("x_hi"), lax.axis_size("x_lo")
     rows, part = mlp_in.shape[1:]
@@ -180,7 +178,6 @@
     with jax.named_scope("gather_z"):
         block = jnp.concatenate([mlp_in[0, :half], mlp_in[0, half:]], axis=1)
         spread = jnp.broadcast_to(block, (n_z, half, 2 * part))
-        spread, place = lax.optimization_barrier((spread, place))
         turned = [[turn(z, n_z) for z in range(n_z)]]
         got = lax.all_to_all(spread, "z", 0, 0, axis_index_groups=turned, tiled=True)
     with jax.named_scope("gather_x"):
@@ -210,20 +207,20 @@
             hidden_kernel,
             "hidden",
             (jax.ShapeDtypeStruct((tokens, width), F32), jax.ShapeDtypeStruct((tokens, lat), BF16)),
-            [SMEM, VMEM, VMEM] + [ANY] * 4,
+            [VMEM, VMEM] + [ANY] * 4,
             [pltpu.VMEM((n_ff, width), BF16) for _ in range(3)]
             + [pltpu.VMEM((lat, width), BF16), dma((4,))],
             6 * tokens * width * n_ff + 2 * tokens * width * lat,
             6 * n_ff * width + 2 * lat * width,
             (VMEM, VMEM),
-        )(place, x, own, gate, up, down, dec)
+        )(x, own, gate, up, down, dec)
     with jax.named_scope("decode"):
         half_sum = (tokens // n_core, width)
         keep, give = call(
             decode_kernel,
             "decode",
             (jax.ShapeDtypeStruct(half_sum, F32), jax.ShapeDtypeStruct(half_sum, BF16)),
-            [SMEM, VMEM, VMEM, ANY],
+            [VMEM, VMEM, ANY],
             [
                 pltpu.VMEM((tokens, width), F32),
                 pltpu.VMEM((layers - 1, lat, width), BF16),
@@ -232,18 +229,18 @@
             6 * tokens * width * lat,
             6 * lat * width,
             (VMEM, VMEM),
-        )(place, every, partial, dec)
+        )(every, partial, dec)
     with jax.named_scope("reduce_core"):
         got = lax.all_gather(give, "core", axis=0, tiled=False)
         send = call(
             join_kernel,
             "join",
             jax.ShapeDtypeStruct((n_hi, n_lo, n_z, half, 2 * part), BF16),
-            [SMEM, VMEM, VMEM],
+            [VMEM, VMEM],
             [],
             0,
             8 * tokens * width,
-        )(place, keep, got)
+        )(keep, got)
     with jax.named_scope("reduce_x"):
         got = lax.all_to_all(send.reshape(n_hi * n_lo, n_z, half, 2 * part), X, 0, 0, tiled=True)
         send = got.astype(F32).sum(0).astype(BF16)

time: 79.2 us -> 78 us (0.985)
  Pallas kernels: 8.47 us -> 6.85 us
  transfers between devices with their start and end apart: 1 -> 1, of which waited for: 1 -> 1; matrix products, arithmetic and copies ran while one was open for 0% -> 0% of each run, Pallas kernels for 4% -> 3%
where the time goes in v7:
time: 78 us; the launch traced here: 77.3 us
  blocking collectives  62.7 us (80%)
  Pallas kernels  6.85 us (9%)
  starting transfers between devices  4.7 us (6%)
  waiting for transfers between devices  1.5 us (2%)
  local copies, waits for them, and re-layouts  0.81 us (1%)
    all_to_all x1, blocking collectives, body(): lax.all_to_all(spread, 'z', 0, 0, axis_index_groups=turned, tiled=True)  22.4 us
    all_to_all x1, blocking collectives, body(): got = lax.all_to_all(send, 'z', 0, 0, axis_index_groups=turned, tiled=True)  15.5 us
    all_to_all x1, blocking collectives, body(): lax.all_to_all(jnp.broadcast_to(got, (n_hi * n_lo,) + got.shape), X, 0, 0...  10.8 us
    all_to_all x1, blocking collectives, body(): lax.all_to_all(send.reshape(n_hi * n_lo, n_z, half, 2 * part), X, 0, 0, t...  9.64 us
    all_to_all x1, starting transfers between devices, body(): every = lax.all_to_all(copies, 'layer', 0, 0, tiled=True)  4.7 us
    pallas_call x1, Pallas kernels, body(): call(hidden_kernel, 'hidden', (jax.ShapeDtypeStruct((tokens, width), F32)...  2.4 us
    all_gather x1, blocking collectives, body(): got = lax.all_gather(give, 'core', axis=0, tiled=False)  2.18 us
    all_gather x1, blocking collectives, body(): got = lax.all_gather(got, 'core', axis=0, tiled=False)  2.17 us
  transfers between devices with their start and end apart: 1, of which 1 were waited for; matrix products, arithmetic and copies ran while one was open for 0% of the time, Pallas kernels for 3%

profile of v7, /device:TPU:24, one launch (start us, length us, event | category | flops | bytes accessed | tf_op | source)
XLA Modules:
  0.0 77.3 jit_solution(4495898006893792145)
XLA Ops:
  0.6 0.0 copy-start
  0.6 0.8 slice_bitcast_fusion.1
  1.4 0.1 pad_maximum_fusion
  1.5 22.4 %all_to_all.25 = bf16[16,16,128]{2,1,0:T(8,128)(2,1)S(1)} all-to-all(bf16[16,16,128]{2,1,0:T(8,128)(2,1)S(1)} %broadcast_in_dim.12), channel_id=1, replica_groups={{16,18,20,22,24,26,28,30,0,2,4,6,8,10,12,14},{17,19,21,23,25,27,29,31,1..., dimensions={0} | all-to-all | bytes 131072 | tf_op jit(solution)/shard_map/gather_z/all_to_all | solution.py:182
  23.9 10.8 %all_to_all.26 = bf16[4,16,16,128]{3,2,1,0:T(8,128)(2,1)S(1)} all-to-all(bf16[4,16,16,128]{3,2,1,0:T(8,128)(2,1)S(1)} %broadcast_in_dim.13), channel_id=1, replica_groups=mesh['layer'=4,'x_lo'=2,'core'=2,'z'=16,'x_hi'=2] {'x_hi','x_lo'}, dimensions={0} | all-to-all | bytes 524288 | tf_op jit(solution)/shard_map/gather_x/all_to_all | solution.py:184
  34.7 2.2 %all-gather = bf16[8,16,16,128]{3,2,1,0:T(8,128)(2,1)S(1)} all-gather(bf16[4,16,16,128]{3,2,1,0:T(8,128)(2,1)S(1)} %all_to_all.26), channel_id=2, replica_groups=mesh['layer'=4,'x_lo'=2,'core'=2,'z'=16,'x_hi'=2] {'core'}, dimensions={0}, use_global_device_ids=true | all-gather | bytes 786432 | tf_op jit(solution)/shard_map/gather_core/all_gather | solution.py:186
  36.8 0.0 copy-done
  36.8 1.6 %encode.1 = (bf16[128,2048]{1,0:T(8,128)(2,1)S(1)}, bf16[128,128]{1,0:T(8,128)(2,1)S(1)}, bf16[4,128,128]{2,1,0:T(8,128)(2,1)}) custom-call(bf16[2,2,2,16,16,128]{5,4,3,2,1,0:T(8,128)(2,1)S(1)} %bitcast.18, bf16[2048,128]{1,0:T(8,128)(2,1)S(1)} %bitcast.21, f32[1,128]{1,0:T(1,128)} %bias.1), custom_call_target="tpu_custom_call" | custom-call | flops 67108864 | bytes 524288 | tf_op jit(solution)/shard_map/encode/encode/pallas_call | solution.py:189
  38.5 4.7 %all-to-all-start.2 = ((bf16[4,128,128]{2,1,0:T(8,128)(2,1)}), bf16[4,128,128]{2,1,0:T(8,128)(2,1)S(1)}, u32[]{:S(2)}, u32[]{:S(2)}) async-start(bf16[4,128,128]{2,1,0:T(8,128)(2,1)} %get-tuple-element.9), calls=%async_computation.2 | async-start | bytes 262144 | tf_op jit(solution)/shard_map/exchange/all_to_all | solution.py:204
  43.2 2.4 %hidden.1 = (f32[128,2048]{1,0:T(8,128)S(1)}, bf16[128,128]{1,0:T(8,128)(2,1)}) custom-call(bf16[128,2048]{1,0:T(8,128)(2,1)S(1)} %get-tuple-element.10.x, bf16[128,128]{1,0:T(8,128)(2,1)S(1)} %get-tuple-element.11.own, bf16[64,2048]{1,0:T(8,128)(2,1)} %bitcast.24, bf16[64,2048]{1,0:T(8,128)(2,1)} %bitcast.25, bf16[64,2048]{1,0:T(8,128)(2,1)} %bitcast.26, ...), custom_call_target="tpu_custom_call" | custom-call | flops 167772160 | bytes 1310720 | tf_op jit(solution)/shard_map/hidden/hidden/pallas_call | solution.py:206
  45.6 1.5 %all-to-all-done.2.got = bf16[4,128,128]{2,1,0:T(8,128)(2,1)S(1)} async-done(((bf16[4,128,128]{2,1,0:T(8,128)(2,1)}), bf16[4,128,128]{2,1,0:T(8,128)(2,1)S(1)}, u32[]{:S(2)}, u32[]{:S(2)}) %all-to-all-start.2) | async-done | bytes 131104 | tf_op jit(solution)/shard_map/exchange/all_to_all | solution.py:204
  47.1 2.0 %decode.1 = (f32[64,2048]{1,0:T(8,128)S(1)}, bf16[64,2048]{1,0:T(8,128)(2,1)S(1)}) custom-call(bf16[4,128,128]{2,1,0:T(8,128)(2,1)S(1)} %all-to-all-done.2.got, f32[128,2048]{1,0:T(8,128)S(1)} %get-tuple-element.12.partial, bf16[4,128,2048]{2,1,0:T(8,128)(2,1)} %bitcast.23), custom_call_target="tpu_custom_call" | custom-call | flops 201326592 | bytes 1572864 | tf_op jit(solution)/shard_map/decode/decode/pallas_call | solution.py:219
  49.1 2.2 %all-gather.1 = bf16[128,2048]{1,0:T(8,128)(2,1)S(1)} all-gather(bf16[64,2048]{1,0:T(8,128)(2,1)S(1)} %get-tuple-element.14), channel_id=3, replica_groups=mesh['layer'=4,'x_lo'=2,'core'=2,'z'=16,'x_hi'=2] {'core'}, dimensions={0}, use_global_device_ids=true | all-gather | bytes 786432 | tf_op jit(solution)/shard_map/reduce_core/all_gather | solution.py:234
  51.3 0.1 join.1
  51.4 9.6 %all_to_all.27 = bf16[4,16,16,128]{3,2,1,0:T(8,128)(2,1)S(1)} all-to-all(bf16[4,16,16,128]{3,2,1,0:T(8,128)(2,1)S(1)} %bitcast.20), channel_id=1, replica_groups=mesh['layer'=4,'x_lo'=2,'core'=2,'z'=16,'x_hi'=2] {'x_hi','x_lo'}, dimensions={0} | all-to-all | bytes 524288 | tf_op jit(solution)/shard_map/reduce_x/all_to_all | solution.py:245
  61.1 15.5 %all_to_all.28.got = bf16[16,16,128]{2,1,0:T(8,128)(2,1)S(1)} all-to-all(bf16[16,16,128]{2,1,0:T(8,128)(2,1)S(1)} %reduce_sum.12), channel_id=1, replica_groups={{16,18,20,22,24,26,28,30,0,2,4,6,8,10,12,14},{17,19,21,23,25,27,29,31,1..., dimensions={0} | all-to-all | bytes 131072 | tf_op jit(solution)/shard_map/reduce_z/all_to_all | solution.py:248
  76.6 0.7 last.1
  (3 shorter events, 0.1 us)
Async XLA Ops:
  0.6 36.2 %copy-start = (bf16[1,2048,128]{2,1,0:T(8,128)(2,1)S(1)}, bf16[1,2048,128]{2,1,0:T(8,128)(2,1)}, u32[]{:S(2)}) copy-start(bf16[1,2048,128]{2,1,0:T(8,128)(2,1)} %param.11) | copy-start | bytes 1572868
  38.5 8.6 %all-to-all-start.2 = ((bf16[4,128,128]{2,1,0:T(8,128)(2,1)}), bf16[4,128,128]{2,1,0:T(8,128)(2,1)S(1)}, u32[]{:S(2)}, u32[]{:S(2)}) async-start(bf16[4,128,128]{2,1,0:T(8,128)(2,1)} %get-tuple-element.9), calls=%async_computation.2 | async-start | bytes 262144 | tf_op jit(solution)/shard_map/exchange/all_to_all | solution.py:204

commit v8 on v7

--- a/solution.py
+++ b/solution.py
@@ -7,7 +7,8 @@
 
 DP = ("x_lo", "core")
 MP = ("z", "x_hi")
-X = ("x_hi", "x_lo")
+X = ("core", "x_hi", "x_lo")
+Z = ("core", "z")
 F32 = jnp.float32
 BF16 = jnp.bfloat16
 VMEM_BYTES = 8 * 2**20
@@ -48,8 +49,20 @@
     return lax.broadcasted_iota(jnp.int32, shape, 1) < shape[1] // 2
 
 
-def turn(z, n_z):
-    return (z + n_z // 2) % n_z
+def z_place(core, z, n_z):
+    return (z + n_z // 2) % n_z if core == 0 else (n_z // 2 - z) % n_z
+
+
+def x_place(core, x, n_x):
+    return x if core == 0 else -x % n_x
+
+
+def groups(place, n_core, n):
+    found = []
+    for core in range(n_core):
+        order = sorted(range(n), key=lambda i: place(core, i, n))
+        found.append([core * n + i for i in order])
+    return found
 
 
 def start_all(sems, pairs):
@@ -66,23 +79,25 @@
 
 
 def encode_kernel(got, enc, bias, x, own, copies, shift, sems):
-    n_core, n_hi, n_lo, n_z, half, lanes = got.shape
+    n_core, n_x, n_z, half, lanes = got.shape
+    n_lo = 2
     loads = start_all(sems, [(bias, shift)])
     low = low_half((half, lanes))
     for lo in range(n_lo):
         for core in range(n_core):
             row = (lo * n_core + core) * 2 * half
             for z in range(n_z):
-                at = turn(z, n_z)
-                a = got[core, 0, lo, at].astype(F32)
-                b = got[core, 1, lo, at].astype(F32)
+                at = z_place(core, z, n_z)
+                a = got[core, x_place(core, lo, n_x), at].astype(F32)
+                b = got[core, x_place(core, n_lo + lo, n_x), at].astype(F32)
                 top = jnp.where(low, a, pltpu.roll(b, lanes // 2, 1))
                 bottom = jnp.where(low, pltpu.roll(a, lanes // 2, 1), b)
                 cols = slice(z * lanes, (z + 1) * lanes)
                 x[row : row + half, cols] = top.astype(BF16)
                 x[row + half : row + 2 * half, cols] = bottom.astype(BF16)
+    pre = dot(x[...], enc[...])
     wait_all(loads)
-    pre = dot(x[...], enc[...]) + shift[...]
+    pre = pre + shift[...]
     value = jnp.maximum(pre, F32(0.0)).astype(BF16)
     own[...] = value
     for s in range(copies.shape[0]):
@@ -141,18 +156,25 @@
 
 
 def join_kernel(keep, got, out):
-    n_hi, n_lo, n_z, half, lanes = out.shape
-    other = 1 - lax.axis_index("core")
+    n_x, n_z, half, lanes = out.shape
+    n_lo = 2
+    core = lax.axis_index("core")
+    other = 1 - core
     low = low_half((half, lanes))
+
+    def pick(place, i, n):
+        return jnp.where(core == 0, place(0, i, n), place(1, i, n))
+
     for lo in range(n_lo):
         row = lo * 2 * half
+        left, right = pick(x_place, lo, n_x), pick(x_place, n_lo + lo, n_x)
         for z in range(n_z):
             cols = slice(z * lanes, (z + 1) * lanes)
             value = keep[row : row + 2 * half, cols] + got[other, row : row + 2 * half, cols].astype(F32)
             top, bottom = value[:half], value[half:]
-            at = turn(z, n_z)
-            out[0, lo, at] = jnp.where(low, top, pltpu.roll(bottom, lanes // 2, 1)).astype(BF16)
-            out[1, lo, at] = jnp.where(low, pltpu.roll(top, lanes // 2, 1), bottom).astype(BF16)
+            at = pick(z_place, z, n_z)
+            out[left, at] = jnp.where(low, top, pltpu.roll(bottom, lanes // 2, 1)).astype(BF16)
+            out[right, at] = jnp.where(low, pltpu.roll(top, lanes // 2, 1), bottom).astype(BF16)
 
 
 def last_kernel(got, out):
@@ -167,6 +189,8 @@
 def body(mlp_in, gate_weight, up_weight, down_weight, enc_weight, enc_bias, dec_weight):
     layers, n_core = lax.axis_size("layer"), lax.axis_size("core")
     n_z, n_hi, n_lo = lax.axis_size("z"), lax.axis_size("x_hi"), lax.axis_size("x_lo")
+    n_x = n_hi * n_lo
+    z_groups, x_groups = groups(z_place, n_core, n_z), groups(x_place, n_core, n_x)
     rows, part = mlp_in.shape[1:]
     half, tokens = rows // 2, rows * n_lo * n_core
     gate, up, down = far(gate_weight[0].T), far(up_weight[0].T), far(down_weight[0])
@@ -178,13 +202,12 @@
     with jax.named_scope("gather_z"):
         block = jnp.concatenate([mlp_in[0, :half], mlp_in[0, half:]], axis=1)
         spread = jnp.broadcast_to(block, (n_z, half, 2 * part))
-        turned = [[turn(z, n_z) for z in range(n_z)]]
-        got = lax.all_to_all(spread, "z", 0, 0, axis_index_groups=turned, tiled=True)
+        got = lax.all_to_all(spread, Z, 0, 0, axis_index_groups=z_groups, tiled=True)
     with jax.named_scope("gather_x"):
-        got = lax.all_to_all(jnp.broadcast_to(got, (n_hi * n_lo,) + got.shape), X, 0, 0, tiled=True)
+        spread = jnp.broadcast_to(got[None], (n_x,) + got.shape)
+        got = lax.all_to_all(spread, X, 0, 0, axis_index_groups=x_groups, tiled=True)
     with jax.named_scope("gather_core"):
         got = lax.all_gather(got, "core", axis=0, tiled=False)
-        got = got.reshape(n_core, n_hi, n_lo, n_z, half, 2 * part)
     with jax.named_scope("encode"):
         x, own, copies = call(
             encode_kernel,
@@ -235,17 +258,17 @@
         send = call(
             join_kernel,
             "join",
-            jax.ShapeDtypeStruct((n_hi, n_lo, n_z, half, 2 * part), BF16),
+            jax.ShapeDtypeStruct((n_x, n_z, half, 2 * part), BF16),
             [VMEM, VMEM],
             [],
             0,
             8 * tokens * width,
         )(keep, got)
     with jax.named_scope("reduce_x"):
-        got = lax.all_to_all(send.reshape(n_hi * n_lo, n_z, half, 2 * part), X, 0, 0, tiled=True)
+        got = lax.all_to_all(send, X, 0, 0, axis_index_groups=x_groups, tiled=True)
         send = got.astype(F32).sum(0).astype(BF16)
     with jax.named_scope("reduce_z"):
-        got = lax.all_to_all(send, "z", 0, 0, axis_index_groups=turned, tiled=True)
+        got = lax.all_to_all(send, Z, 0, 0, axis_index_groups=z_groups, tiled=True)
     with jax.named_scope("last"):
         error = call(
             last_kernel,

time: 78 us -> 78 us (level)
  no operation moved by 1% of the time
where the time goes in v8:
time: 78 us; the launch traced here: 77.3 us
  blocking collectives  62.7 us (80%)
  Pallas kernels  6.84 us (9%)
  starting transfers between devices  4.7 us (6%)
  waiting for transfers between devices  1.5 us (2%)
  local copies, waits for them, and re-layouts  0.81 us (1%)
    all_to_all x1, blocking collectives, body(): lax.all_to_all(spread, Z, 0, 0, axis_index_groups=z_groups, tiled=True)  22.4 us
    all_to_all x1, blocking collectives, body(): got = lax.all_to_all(send, Z, 0, 0, axis_index_groups=z_groups, tiled=True)  15.5 us
    all_to_all x1, blocking collectives, body(): lax.all_to_all(spread, X, 0, 0, axis_index_groups=x_groups, tiled=True)  10.8 us
    all_to_all x1, blocking collectives, body(): got = lax.all_to_all(send, X, 0, 0, axis_index_groups=x_groups, tiled=True)  9.64 us
    all_to_all x1, starting transfers between devices, body(): every = lax.all_to_all(copies, 'layer', 0, 0, tiled=True)  4.7 us
    pallas_call x1, Pallas kernels, body(): call(hidden_kernel, 'hidden', (jax.ShapeDtypeStruct((tokens, width), F32)...  2.4 us
    all_gather x1, blocking collectives, body(): got = lax.all_gather(give, 'core', axis=0, tiled=False)  2.18 us
    all_gather x1, blocking collectives, body(): got = lax.all_gather(got, 'core', axis=0, tiled=False)  2.17 us
  transfers between devices with their start and end apart: 1, of which 1 were waited for; matrix products, arithmetic and copies ran while one was open for 0% of the time, Pallas kernels for 3%

profile of v8, /device:TPU:24, one launch (start us, length us, event | category | flops | bytes accessed | tf_op | source)
XLA Modules:
  0.0 77.3 jit_solution(14451419996494709528)
XLA Ops:
  0.6 0.0 copy-start
  0.6 0.8 slice_bitcast_fusion.1
  1.4 0.1 pad_maximum_fusion
  1.5 22.4 %all_to_all.25 = bf16[16,16,128]{2,1,0:T(8,128)(2,1)S(1)} all-to-all(bf16[16,16,128]{2,1,0:T(8,128)(2,1)S(1)} %broadcast_in_dim.15), channel_id=1, replica_groups={{16,18,20,22,24,26,28,30,0,2,4,6,8,10,12,14},{48,46,44,42,40,38,36,34,3..., dimensions={0} | all-to-all | bytes 131072 | tf_op jit(solution)/shard_map/gather_z/all_to_all | solution.py:205
  23.9 10.8 %all_to_all.26 = bf16[4,16,16,128]{3,2,1,0:T(8,128)(2,1)S(1)} all-to-all(bf16[4,16,16,128]{3,2,1,0:T(8,128)(2,1)S(1)} %broadcast_in_dim.16), channel_id=1, replica_groups={{0,64,1,65},{32,97,33,96},{2,66,3,67},{34,99,35,98},{4,68,5,69},{36,101..., dimensions={0} | all-to-all | bytes 524288 | tf_op jit(solution)/shard_map/gather_x/all_to_all | solution.py:208
  34.7 2.2 %all-gather = bf16[8,16,16,128]{3,2,1,0:T(8,128)(2,1)S(1)} all-gather(bf16[4,16,16,128]{3,2,1,0:T(8,128)(2,1)S(1)} %all_to_all.26), channel_id=2, replica_groups=mesh['layer'=4,'x_lo'=2,'core'=2,'z'=16,'x_hi'=2] {'core'}, dimensions={0}, use_global_device_ids=true | all-gather | bytes 786432 | tf_op jit(solution)/shard_map/gather_core/all_gather | solution.py:210
  36.8 0.0 copy-done
  36.8 1.6 %encode.1 = (bf16[128,2048]{1,0:T(8,128)(2,1)S(1)}, bf16[128,128]{1,0:T(8,128)(2,1)S(1)}, bf16[4,128,128]{2,1,0:T(8,128)(2,1)}) custom-call(bf16[2,4,16,16,128]{4,3,2,1,0:T(8,128)(2,1)S(1)} %bitcast.17, bf16[2048,128]{1,0:T(8,128)(2,1)S(1)} %bitcast.19, f32[1,128]{1,0:T(1,128)} %bias.1), custom_call_target="tpu_custom_call" | custom-call | flops 67108864 | bytes 524288 | tf_op jit(solution)/shard_map/encode/encode/pallas_call | solution.py:212
  38.5 4.7 %all-to-all-start.2 = ((bf16[4,128,128]{2,1,0:T(8,128)(2,1)}), bf16[4,128,128]{2,1,0:T(8,128)(2,1)S(1)}, u32[]{:S(2)}, u32[]{:S(2)}) async-start(bf16[4,128,128]{2,1,0:T(8,128)(2,1)} %get-tuple-element.9), calls=%async_computation.2 | async-start | bytes 262144 | tf_op jit(solution)/shard_map/exchange/all_to_all | solution.py:227
  43.2 2.4 %hidden.1 = (f32[128,2048]{1,0:T(8,128)S(1)}, bf16[128,128]{1,0:T(8,128)(2,1)}) custom-call(bf16[128,2048]{1,0:T(8,128)(2,1)S(1)} %get-tuple-element.10.x, bf16[128,128]{1,0:T(8,128)(2,1)S(1)} %get-tuple-element.11.own, bf16[64,2048]{1,0:T(8,128)(2,1)} %bitcast.22, bf16[64,2048]{1,0:T(8,128)(2,1)} %bitcast.23, bf16[64,2048]{1,0:T(8,128)(2,1)} %bitcast.24, ...), custom_call_target="tpu_custom_call" | custom-call | flops 167772160 | bytes 1310720 | tf_op jit(solution)/shard_map/hidden/hidden/pallas_call | solution.py:229
  45.6 1.5 %all-to-all-done.2.got = bf16[4,128,128]{2,1,0:T(8,128)(2,1)S(1)} async-done(((bf16[4,128,128]{2,1,0:T(8,128)(2,1)}), bf16[4,128,128]{2,1,0:T(8,128)(2,1)S(1)}, u32[]{:S(2)}, u32[]{:S(2)}) %all-to-all-start.2) | async-done | bytes 131104 | tf_op jit(solution)/shard_map/exchange/all_to_all | solution.py:227
  47.1 2.0 %decode.1 = (f32[64,2048]{1,0:T(8,128)S(1)}, bf16[64,2048]{1,0:T(8,128)(2,1)S(1)}) custom-call(bf16[4,128,128]{2,1,0:T(8,128)(2,1)S(1)} %all-to-all-done.2.got, f32[128,2048]{1,0:T(8,128)S(1)} %get-tuple-element.12.partial, bf16[4,128,2048]{2,1,0:T(8,128)(2,1)} %bitcast.21), custom_call_target="tpu_custom_call" | custom-call | flops 201326592 | bytes 1572864 | tf_op jit(solution)/shard_map/decode/decode/pallas_call | solution.py:242
  49.1 2.2 %all-gather.1 = bf16[128,2048]{1,0:T(8,128)(2,1)S(1)} all-gather(bf16[64,2048]{1,0:T(8,128)(2,1)S(1)} %get-tuple-element.14), channel_id=3, replica_groups=mesh['layer'=4,'x_lo'=2,'core'=2,'z'=16,'x_hi'=2] {'core'}, dimensions={0}, use_global_device_ids=true | all-gather | bytes 786432 | tf_op jit(solution)/shard_map/reduce_core/all_gather | solution.py:257
  51.3 0.1 join.1
  51.4 9.6 %all_to_all.27 = bf16[4,16,16,128]{3,2,1,0:T(8,128)(2,1)S(1)} all-to-all(bf16[4,16,16,128]{3,2,1,0:T(8,128)(2,1)S(1)} %join.1), channel_id=1, replica_groups={{0,64,1,65},{32,97,33,96},{2,66,3,67},{34,99,35,98},{4,68,5,69},{36,101..., dimensions={0} | all-to-all | bytes 524288 | tf_op jit(solution)/shard_map/reduce_x/all_to_all | solution.py:268
  61.1 15.5 %all_to_all.28.got = bf16[16,16,128]{2,1,0:T(8,128)(2,1)S(1)} all-to-all(bf16[16,16,128]{2,1,0:T(8,128)(2,1)S(1)} %reduce_sum.12), channel_id=1, replica_groups={{16,18,20,22,24,26,28,30,0,2,4,6,8,10,12,14},{48,46,44,42,40,38,36,34,3..., dimensions={0} | all-to-all | bytes 131072 | tf_op jit(solution)/shard_map/reduce_z/all_to_all | solution.py:271
  76.6 0.7 last.1
  (3 shorter events, 0.1 us)
Async XLA Ops:
  0.6 36.2 %copy-start = (bf16[1,2048,128]{2,1,0:T(8,128)(2,1)S(1)}, bf16[1,2048,128]{2,1,0:T(8,128)(2,1)}, u32[]{:S(2)}) copy-start(bf16[1,2048,128]{2,1,0:T(8,128)(2,1)} %param.11) | copy-start | bytes 1572868
  38.5 8.6 %all-to-all-start.2 = ((bf16[4,128,128]{2,1,0:T(8,128)(2,1)}), bf16[4,128,128]{2,1,0:T(8,128)(2,1)S(1)}, u32[]{:S(2)}, u32[]{:S(2)}) async-start(bf16[4,128,128]{2,1,0:T(8,128)(2,1)} %get-tuple-element.9), calls=%async_computation.2 | async-start | bytes 262144 | tf_op jit(solution)/shard_map/exchange/all_to_all | solution.py:227

commit v9 on v3

--- a/solution.py
+++ b/solution.py
@@ -12,7 +12,6 @@
 BF16 = jnp.bfloat16
 VMEM_BYTES = 8 * 2**20
 VMEM = pl.BlockSpec(memory_space=pltpu.VMEM)
-SMEM = pl.BlockSpec(memory_space=pltpu.SMEM)
 ANY = pl.BlockSpec(memory_space=pl.ANY)
 
 
@@ -67,19 +66,12 @@
 
 
 def front_kernel(
-    place, got, enc, bias, gate, up, down, dec, latent, copies, out, x, encs, shift, gates, ups, downs, decs, sems
+    got, enc, dec, bias, gate, up, down, own, latent, out, x, shift, gates, ups, downs, decs, sems
 ):
     n_core, n_hi, n_lo, n_z, half, lanes = got.shape
     loads = start_all(
         sems,
-        [
-            (enc, encs),
-            (bias, shift),
-            (gate, gates),
-            (up, ups),
-            (down, downs),
-            (dec.at[place[0]], decs),
-        ],
+        [(bias, shift), (gate, gates), (up, ups), (down, downs), (dec.at[lax.axis_index("layer")], decs)],
     )
     low = low_half((half, lanes))
     for lo in range(n_lo):
@@ -95,48 +87,32 @@
                 x[row : row + half, cols] = top.astype(BF16)
                 x[row + half : row + 2 * half, cols] = bottom.astype(BF16)
     rows = x[...]
-    wait_all(loads[:2])
-    pre = dot(rows, encs[...]) + shift[...]
-    value = jnp.maximum(pre, F32(0.0)).astype(BF16)
+    pre = dot(rows, enc[...])
+    wait_all(loads)
+    value = jnp.maximum(pre + shift[...], F32(0.0)).astype(BF16)
+    own[...] = value
     latent[...] = value
-    for s in range(copies.shape[0]):
-        copies[s] = value
-    wait_all(loads[2:4])
     gate_part = dot_t(rows, gates[...])
     up_part = dot_t(rows, ups[...])
     hidden = (gate_part / (1.0 + jnp.exp(-gate_part)) * up_part).astype(BF16)
-    wait_all(loads[4:])
     tile = 256
     for n in range(0, x.shape[1], tile):
         cols = slice(n, n + tile)
         out[:, cols] = dot(hidden, downs[:, cols]) - dot(value, decs[:, cols])
 
 
-def decode_kernel(place, got, partial, dec, keep, give, total, decs, sems):
-    n_src = got.shape[0]
-    layer, core = place[0], place[1]
-
-    def load(back):
-        return pltpu.make_async_copy(dec.at[layer - back], decs.at[back - 1], sems.at[back - 1])
-
-    for back in range(1, n_src):
+def decode_kernel(got, partial, dec, keep, give, total):
+    layer, core = lax.axis_index("layer"), lax.axis_index("core")
+    total[...] = partial[...]
+    tile = 256
+    for back in range(1, got.shape[0]):
 
         @pl.when(layer >= back)
         def _():
-            load(back).start()
-
-    total[...] = partial[...]
-    tile = 256
-    for back in range(1, n_src):
-
-        @pl.when(layer >= back)
-        def _():
-            load(back).wait()
             rows = got[layer - back]
             for n in range(0, total.shape[1], tile):
-                total[:, n : n + tile] = total[:, n : n + tile] - dot(
-                    rows, decs[back - 1, :, n : n + tile]
-                )
+                cols = slice(n, n + tile)
+                total[:, cols] = total[:, cols] - dot(rows, dec[layer - back, :, cols])
 
     rows = keep.shape[0] // 2
     for lo in range(2):
@@ -146,9 +122,9 @@
         give[lo * rows : (lo + 1) * rows] = total[pl.ds(theirs, rows)].astype(BF16)
 
 
-def join_kernel(place, keep, got, out):
+def join_kernel(keep, got, out):
     n_hi, n_lo, n_z, half, lanes = out.shape
-    other = 1 - place[1]
+    other = 1 - lax.axis_index("core")
     low = low_half((half, lanes))
     for lo in range(n_lo):
         row = lo * 2 * half
@@ -171,20 +147,19 @@
 
 
 def body(mlp_in, gate_weight, up_weight, down_weight, enc_weight, enc_bias, dec_weight):
-    place = jnp.stack([lax.axis_index("layer"), lax.axis_index("core")]).astype(jnp.int32)
     layers, n_core = lax.axis_size("layer"), lax.axis_size("core")
     n_z, n_hi, n_lo = lax.axis_size("z"), lax.axis_size("x_hi"), lax.axis_size("x_lo")
     rows, part = mlp_in.shape[1:]
     half, tokens = rows // 2, rows * n_lo * n_core
     gate, up, down = far(gate_weight[0].T), far(up_weight[0].T), far(down_weight[0])
-    enc, dec = far(enc_weight[0]), far(dec_weight[0])
+    enc = pltpu.with_memory_space_constraint(enc_weight[0], pltpu.VMEM)
+    dec = pltpu.with_memory_space_constraint(dec_weight[0], pltpu.VMEM)
     width, lat = enc.shape
     n_ff = gate.shape[0]
     dma = pltpu.SemaphoreType.DMA
     with jax.named_scope("gather_z"):
         block = jnp.concatenate([mlp_in[0, :half], mlp_in[0, half:]], axis=1)
         spread = jnp.broadcast_to(block, (n_z, half, 2 * part))
-        spread, place = lax.optimization_barrier((spread, place))
         turned = [[turn(z, n_z) for z in range(n_z)]]
         got = lax.all_to_all(spread, "z", 0, 0, axis_index_groups=turned, tiled=True)
     with jax.named_scope("gather_x"):
@@ -193,51 +168,47 @@
         got = lax.all_gather(got, "core", axis=0, tiled=False)
         got = got.reshape(n_core, n_hi, n_lo, n_z, half, 2 * part)
     with jax.named_scope("front"):
-        latent, copies, partial = call(
+        own, latent, partial = call(
             front_kernel,
             "front",
             (
                 jax.ShapeDtypeStruct((tokens, lat), BF16),
-                jax.ShapeDtypeStruct((layers, tokens, lat), BF16),
+                jax.ShapeDtypeStruct((tokens, lat), BF16),
                 jax.ShapeDtypeStruct((tokens, width), F32),
             ),
-            [SMEM, VMEM] + [ANY] * 6,
-            [pltpu.VMEM((tokens, width), BF16), pltpu.VMEM((width, lat), BF16), pltpu.VMEM((1, lat), F32)]
+            [VMEM] * 2 + [ANY] * 5,
+            [pltpu.VMEM((tokens, width), BF16), pltpu.VMEM((1, lat), F32)]
             + [pltpu.VMEM((n_ff, width), BF16) for _ in range(3)]
-            + [pltpu.VMEM((lat, width), BF16), dma((6,))],
+            + [pltpu.VMEM((lat, width), BF16), dma((5,))],
             6 * tokens * width * n_ff + 4 * tokens * width * lat,
             6 * n_ff * width + 4 * lat * width,
             (VMEM, VMEM, VMEM),
-        )(place, got, enc, far(enc_bias), gate, up, down, dec)
+        )(got, enc, far(dec_weight[0]), far(enc_bias), gate, up, down)
     with jax.named_scope("exchange"):
-        every = lax.all_to_all(copies, "layer", 0, 0, tiled=True)
+        every = lax.all_gather(own, "layer", axis=0, tiled=False)
     with jax.named_scope("decode"):
         half_sum = (tokens // n_core, width)
         keep, give = call(
             decode_kernel,
             "decode",
             (jax.ShapeDtypeStruct(half_sum, F32), jax.ShapeDtypeStruct(half_sum, BF16)),
-            [SMEM, VMEM, VMEM, ANY],
-            [
-                pltpu.VMEM((tokens, width), F32),
-                pltpu.VMEM((layers - 1, lat, width), BF16),
-                dma((layers - 1,)),
-            ],
+            [VMEM, VMEM, VMEM],
+            [pltpu.VMEM((tokens, width), F32)],
             6 * tokens * width * lat,
             6 * lat * width,
             (VMEM, VMEM),
-        )(place, every, partial, dec)
+        )(every, partial, dec)
     with jax.named_scope("reduce_core"):
         got = lax.all_gather(give, "core", axis=0, tiled=False)
         send = call(
             join_kernel,
             "join",
             jax.ShapeDtypeStruct((n_hi, n_lo, n_z, half, 2 * part), BF16),
-            [SMEM, VMEM, VMEM],
+            [VMEM, VMEM],
             [],
             0,
             8 * tokens * width,
-        )(place, keep, got)
+        )(keep, got)
     with jax.named_scope("reduce_x"):
         got = lax.all_to_all(send.reshape(n_hi * n_lo, n_z, half, 2 * part), X, 0, 0, tiled=True)
         send = got.astype(F32).sum(0).astype(BF16)

time: 80.2 us -> 80.8 us (level)
  blocking collectives: 71 us -> 74.7 us
  Pallas kernels: 6.89 us -> 4.26 us
    all_gather x0 -> x1, blocking collectives: none -> 12 us  [body(): every = lax.all_gather(own, 'layer', axis=0, tiled=False)]
    all_to_all x1 -> x0, blocking collectives: 8.4 us -> none  [body(): every = lax.all_to_all(copies, 'layer', 0, 0, tiled=True)]
    pallas_call x1, Pallas kernels: 2.54 us -> 0.99 us  [body(): call(decode_kernel, 'decode', (jax.ShapeDtypeStruct(half_sum, F32), jax.S...]
where the time goes in v9:
time: 80.8 us; the launch traced here: 80.5 us
  blocking collectives  74.7 us (92%)
  Pallas kernels  4.26 us (5%)
  local copies, waits for them, and re-layouts  0.82 us (1%)
    all_to_all x1, blocking collectives, body(): lax.all_to_all(spread, 'z', 0, 0, axis_index_groups=turned, tiled=True)  22.4 us
    all_to_all x1, blocking collectives, body(): got = lax.all_to_all(send, 'z', 0, 0, axis_index_groups=turned, tiled=True)  15.6 us
    all_gather x1, blocking collectives, body(): every = lax.all_gather(own, 'layer', axis=0, tiled=False)  12 us
    all_to_all x1, blocking collectives, body(): lax.all_to_all(jnp.broadcast_to(got, (n_hi * n_lo,) + got.shape), X, 0, 0...  10.8 us
    all_to_all x1, blocking collectives, body(): lax.all_to_all(send.reshape(n_hi * n_lo, n_z, half, 2 * part), X, 0, 0, t...  9.64 us
    pallas_call x1, Pallas kernels, body(): call(front_kernel, 'front', (jax.ShapeDtypeStruct((tokens, lat), BF16), j...  2.44 us
    all_gather x1, blocking collectives, body(): got = lax.all_gather(give, 'core', axis=0, tiled=False)  2.18 us
    all_gather x1, blocking collectives, body(): got = lax.all_gather(got, 'core', axis=0, tiled=False)  2.17 us

profile of v9, /device:TPU:24, one launch (start us, length us, event | category | flops | bytes accessed | tf_op | source)
XLA Modules:
  0.0 80.5 jit_solution(17983835700415617100)
XLA Ops:
  0.6 0.0 copy-start.1
  0.6 0.8 slice_bitcast_fusion.1
  1.4 0.1 pad_maximum_fusion
  1.5 22.4 %all_to_all.20 = bf16[16,16,128]{2,1,0:T(8,128)(2,1)S(1)} all-to-all(bf16[16,16,128]{2,1,0:T(8,128)(2,1)S(1)} %broadcast_in_dim.12), channel_id=1, replica_groups={{16,18,20,22,24,26,28,30,0,2,4,6,8,10,12,14},{17,19,21,23,25,27,29,31,1..., dimensions={0} | all-to-all | bytes 131072 | tf_op jit(solution)/shard_map/gather_z/all_to_all | solution.py:164
  23.9 10.8 %all_to_all.21 = bf16[4,16,16,128]{3,2,1,0:T(8,128)(2,1)S(1)} all-to-all(bf16[4,16,16,128]{3,2,1,0:T(8,128)(2,1)S(1)} %broadcast_in_dim.13), channel_id=1, replica_groups=mesh['layer'=4,'x_lo'=2,'core'=2,'z'=16,'x_hi'=2] {'x_hi','x_lo'}, dimensions={0} | all-to-all | bytes 524288 | tf_op jit(solution)/shard_map/gather_x/all_to_all | solution.py:166
  34.7 2.2 %all-gather = bf16[8,16,16,128]{3,2,1,0:T(8,128)(2,1)S(1)} all-gather(bf16[4,16,16,128]{3,2,1,0:T(8,128)(2,1)S(1)} %all_to_all.21), channel_id=2, replica_groups=mesh['layer'=4,'x_lo'=2,'core'=2,'z'=16,'x_hi'=2] {'core'}, dimensions={0}, use_global_device_ids=true | all-gather | bytes 786432 | tf_op jit(solution)/shard_map/gather_core/all_gather | solution.py:168
  36.8 0.0 copy-start
  36.8 0.0 copy-done.1
  36.8 2.4 %front.1 = (bf16[128,128]{1,0:T(8,128)(2,1)S(1)}, bf16[128,128]{1,0:T(8,128)(2,1)}, f32[128,2048]{1,0:T(8,128)S(1)}) custom-call(bf16[2,2,2,16,16,128]{5,4,3,2,1,0:T(8,128)(2,1)S(1)} %bitcast.21, bf16[2048,128]{1,0:T(8,128)(2,1)S(1)} %bitcast.24, bf16[4,128,2048]{2,1,0:T(8,128)(2,1)} %bitcast.19, f32[1,128]{1,0:T(1,128)} %bias.1, bf16[64,2048]{1,0:T(8,128)(2,1)} %bitcast.26, ...), custom_call_target="tpu_custom_call" | custom-call | flops 234881024 | bytes 1835008 | tf_op jit(solution)/shard_map/front/front/pallas_call | solution.py:171
  39.3 12.0 %all-gather.1 = bf16[512,128]{1,0:T(8,128)(2,1)S(1)} all-gather(bf16[128,128]{1,0:T(8,128)(2,1)S(1)} %get-tuple-element.7), channel_id=3, replica_groups=mesh['layer'=4,'x_lo'=2,'core'=2,'z'=16,'x_hi'=2] {'layer'}, dimensions={0}, use_global_device_ids=true | all-gather | bytes 163840 | tf_op jit(solution)/shard_map/exchange/all_gather | solution.py:188
  51.3 0.0 copy-done
  51.3 1.0 %decode.1 = (f32[64,2048]{1,0:T(8,128)S(1)}, bf16[64,2048]{1,0:T(8,128)(2,1)S(1)}) custom-call(bf16[4,128,128]{2,1,0:T(8,128)(2,1)S(1)} %bitcast.25, f32[128,2048]{1,0:T(8,128)S(1)} %get-tuple-element.8.partial, bf16[4,128,2048]{2,1,0:T(8,128)(2,1)S(1)} %bitcast.20), custom_call_target="tpu_custom_call" | custom-call | flops 201326592 | bytes 1572864 | tf_op jit(solution)/shard_map/decode/decode/pallas_call | solution.py:191
  52.3 2.2 %all-gather.2 = bf16[128,2048]{1,0:T(8,128)(2,1)S(1)} all-gather(bf16[64,2048]{1,0:T(8,128)(2,1)S(1)} %get-tuple-element.10), channel_id=4, replica_groups=mesh['layer'=4,'x_lo'=2,'core'=2,'z'=16,'x_hi'=2] {'core'}, dimensions={0}, use_global_device_ids=true | all-gather | bytes 786432 | tf_op jit(solution)/shard_map/reduce_core/all_gather | solution.py:202
  54.5 0.1 join.1
  54.6 9.6 %all_to_all.22 = bf16[4,16,16,128]{3,2,1,0:T(8,128)(2,1)S(1)} all-to-all(bf16[4,16,16,128]{3,2,1,0:T(8,128)(2,1)S(1)} %bitcast.23), channel_id=1, replica_groups=mesh['layer'=4,'x_lo'=2,'core'=2,'z'=16,'x_hi'=2] {'x_hi','x_lo'}, dimensions={0} | all-to-all | bytes 524288 | tf_op jit(solution)/shard_map/reduce_x/all_to_all | solution.py:213
  64.3 15.6 %all_to_all.23.got = bf16[16,16,128]{2,1,0:T(8,128)(2,1)S(1)} all-to-all(bf16[16,16,128]{2,1,0:T(8,128)(2,1)S(1)} %reduce_sum.12), channel_id=1, replica_groups={{16,18,20,22,24,26,28,30,0,2,4,6,8,10,12,14},{17,19,21,23,25,27,29,31,1..., dimensions={0} | all-to-all | bytes 131072 | tf_op jit(solution)/shard_map/reduce_z/all_to_all | solution.py:216
  79.8 0.7 last.1
  (3 shorter events, 0.1 us)
Async XLA Ops:
  0.6 36.2 %copy-start.1 = (bf16[1,2048,128]{2,1,0:T(8,128)(2,1)S(1)}, bf16[1,2048,128]{2,1,0:T(8,128)(2,1)}, u32[]{:S(2)}) copy-start(bf16[1,2048,128]{2,1,0:T(8,128)(2,1)} %param.11) | copy-start | bytes 1572868
  36.8 14.5 %copy-start = (bf16[1,4,128,2048]{3,2,1,0:T(8,128)(2,1)S(1)}, bf16[1,4,128,2048]{3,2,1,0:T(8,128)(2,1)}, u32[]{:S(2)}) copy-start(bf16[1,4,128,2048]{3,2,1,0:T(8,128)(2,1)} %param.13) | copy-start | bytes 6291460

commit v10 on v7

--- a/solution.py
+++ b/solution.py
@@ -106,31 +106,18 @@
         out[:, cols] = dot(hidden, downs[:, cols]) - dot(own[...], decs[:, cols])
 
 
-def decode_kernel(got, partial, dec, keep, give, total, decs, sems):
-    n_src = got.shape[0]
+def decode_kernel(got, partial, dec, keep, give, total):
     layer, core = lax.axis_index("layer"), lax.axis_index("core")
-
-    def load(back):
-        return pltpu.make_async_copy(dec.at[layer - back], decs.at[back - 1], sems.at[back - 1])
-
-    for back in range(1, n_src):
+    total[...] = partial[...]
+    tile = 256
+    for back in range(1, got.shape[0]):
 
         @pl.when(layer >= back)
         def _():
-            load(back).start()
-
-    total[...] = partial[...]
-    tile = 256
-    for back in range(1, n_src):
-
-        @pl.when(layer >= back)
-        def _():
-            load(back).wait()
             rows = got[layer - back]
             for n in range(0, total.shape[1], tile):
-                total[:, n : n + tile] = total[:, n : n + tile] - dot(
-                    rows, decs[back - 1, :, n : n + tile]
-                )
+                cols = slice(n, n + tile)
+                total[:, cols] = total[:, cols] - dot(rows, dec[layer - back, :, cols])
 
     rows = keep.shape[0] // 2
     for lo in range(2):
@@ -220,16 +207,12 @@
             decode_kernel,
             "decode",
             (jax.ShapeDtypeStruct(half_sum, F32), jax.ShapeDtypeStruct(half_sum, BF16)),
-            [VMEM, VMEM, ANY],
-            [
-                pltpu.VMEM((tokens, width), F32),
-                pltpu.VMEM((layers - 1, lat, width), BF16),
-                dma((layers - 1,)),
-            ],
+            [VMEM, VMEM, VMEM],
+            [pltpu.VMEM((tokens, width), F32)],
             6 * tokens * width * lat,
             6 * lat * width,
             (VMEM, VMEM),
-        )(every, partial, dec)
+        )(every, partial, pltpu.with_memory_space_constraint(dec_weight[0, : layers - 1], pltpu.VMEM))
     with jax.named_scope("reduce_core"):
         got = lax.all_gather(give, "core", axis=0, tiled=False)
         send = call(

time: 78 us -> 77.2 us (0.990)
  local copies, waits for them, and re-layouts: 0.81 us -> 2.32 us
  waiting for transfers between devices: 1.5 us -> 0.01 us
  Pallas kernels: 6.85 us -> 5.86 us
    squeeze x0 -> x1, local copies, waits for them, and re-layouts: none -> 1.51 us  [body(): dec_weight[0, :layers - 1]]
    all_to_all x1, waiting for transfers between devices: 1.5 us -> 0.01 us  [body(): every = lax.all_to_all(copies, 'layer', 0, 0, tiled=True)]
    pallas_call x1, Pallas kernels: 2 us -> 0.99 us  [body(): call(decode_kernel, 'decode', (jax.ShapeDtypeStruct(half_sum, F32), jax.S...]
  transfers between devices with their start and end apart: 1 -> 1, of which waited for: 1 -> 0; matrix products, arithmetic and copies ran while one was open for 0% -> 2% of each run, Pallas kernels for 3% -> 3%
where the time goes in v10:
time: 77.2 us; the launch traced here: 76.3 us
  blocking collectives  62.6 us (81%)
  Pallas kernels  5.86 us (8%)
  starting transfers between devices  4.7 us (6%)
  local copies, waits for them, and re-layouts  2.32 us (3%)
    all_to_all x1, blocking collectives, body(): lax.all_to_all(spread, 'z', 0, 0, axis_index_groups=turned, tiled=True)  22.4 us
    all_to_all x1, blocking collectives, body(): got = lax.all_to_all(send, 'z', 0, 0, axis_index_groups=turned, tiled=True)  15.5 us
    all_to_all x1, blocking collectives, body(): lax.all_to_all(jnp.broadcast_to(got, (n_hi * n_lo,) + got.shape), X, 0, 0...  10.8 us
    all_to_all x1, blocking collectives, body(): lax.all_to_all(send.reshape(n_hi * n_lo, n_z, half, 2 * part), X, 0, 0, t...  9.64 us
    all_to_all x1, starting transfers between devices, body(): every = lax.all_to_all(copies, 'layer', 0, 0, tiled=True)  4.7 us
    pallas_call x1, Pallas kernels, body(): call(hidden_kernel, 'hidden', (jax.ShapeDtypeStruct((tokens, width), F32)...  2.41 us
    all_gather x1, blocking collectives, body(): got = lax.all_gather(give, 'core', axis=0, tiled=False)  2.18 us
    all_gather x1, blocking collectives, body(): got = lax.all_gather(got, 'core', axis=0, tiled=False)  2.17 us
  transfers between devices with their start and end apart: 1, of which 0 were waited for; matrix products, arithmetic and copies ran while one was open for 2% of the time, Pallas kernels for 3%

profile of v10, /device:TPU:24, one launch (start us, length us, event | category | flops | bytes accessed | tf_op | source)
XLA Modules:
  0.0 76.3 jit_solution(13697532612558333379)
XLA Ops:
  0.6 0.0 copy-start
  0.6 0.8 slice_bitcast_fusion.2
  1.4 0.1 pad_maximum_fusion
  1.5 22.4 %all_to_all.25 = bf16[16,16,128]{2,1,0:T(8,128)(2,1)S(1)} all-to-all(bf16[16,16,128]{2,1,0:T(8,128)(2,1)S(1)} %broadcast_in_dim.12), channel_id=1, replica_groups={{16,18,20,22,24,26,28,30,0,2,4,6,8,10,12,14},{17,19,21,23,25,27,29,31,1..., dimensions={0} | all-to-all | bytes 131072 | tf_op jit(solution)/shard_map/gather_z/all_to_all | solution.py:169
  23.9 10.8 %all_to_all.26 = bf16[4,16,16,128]{3,2,1,0:T(8,128)(2,1)S(1)} all-to-all(bf16[4,16,16,128]{3,2,1,0:T(8,128)(2,1)S(1)} %broadcast_in_dim.13), channel_id=1, replica_groups=mesh['layer'=4,'x_lo'=2,'core'=2,'z'=16,'x_hi'=2] {'x_hi','x_lo'}, dimensions={0} | all-to-all | bytes 524288 | tf_op jit(solution)/shard_map/gather_x/all_to_all | solution.py:171
  34.7 2.2 %all-gather = bf16[8,16,16,128]{3,2,1,0:T(8,128)(2,1)S(1)} all-gather(bf16[4,16,16,128]{3,2,1,0:T(8,128)(2,1)S(1)} %all_to_all.26), channel_id=2, replica_groups=mesh['layer'=4,'x_lo'=2,'core'=2,'z'=16,'x_hi'=2] {'core'}, dimensions={0}, use_global_device_ids=true | all-gather | bytes 786432 | tf_op jit(solution)/shard_map/gather_core/all_gather | solution.py:173
  36.8 0.0 copy-done
  36.8 1.6 %encode.1 = (bf16[128,2048]{1,0:T(8,128)(2,1)S(1)}, bf16[128,128]{1,0:T(8,128)(2,1)S(1)}, bf16[4,128,128]{2,1,0:T(8,128)(2,1)}) custom-call(bf16[2,2,2,16,16,128]{5,4,3,2,1,0:T(8,128)(2,1)S(1)} %bitcast.20, bf16[2048,128]{1,0:T(8,128)(2,1)S(1)} %bitcast.23, f32[1,128]{1,0:T(1,128)} %bias.1), custom_call_target="tpu_custom_call" | custom-call | flops 67108864 | bytes 524288 | tf_op jit(solution)/shard_map/encode/encode/pallas_call | solution.py:176
  38.5 4.7 %all-to-all-start.2 = ((bf16[4,128,128]{2,1,0:T(8,128)(2,1)}), bf16[4,128,128]{2,1,0:T(8,128)(2,1)S(1)}, u32[]{:S(2)}, u32[]{:S(2)}) async-start(bf16[4,128,128]{2,1,0:T(8,128)(2,1)} %get-tuple-element.9), calls=%async_computation.2 | async-start | bytes 262144 | tf_op jit(solution)/shard_map/exchange/all_to_all | solution.py:191
  43.2 1.5 %slice_bitcast_fusion.dec = bf16[3,128,2048]{2,1,0:T(8,128)(2,1)S(1)} fusion(bf16[1,4,128,2048]{3,2,1,0:T(8,128)(2,1)} %param.13), kind=kLoop, calls=%fused_computation | loop fusion | bytes 3145728 | tf_op jit(solution)/shard_map/decode/squeeze | solution.py:215
  44.7 2.4 %hidden.1 = (f32[128,2048]{1,0:T(8,128)S(1)}, bf16[128,128]{1,0:T(8,128)(2,1)}) custom-call(bf16[128,2048]{1,0:T(8,128)(2,1)S(1)} %get-tuple-element.10.x, bf16[128,128]{1,0:T(8,128)(2,1)S(1)} %get-tuple-element.11.own, bf16[64,2048]{1,0:T(8,128)(2,1)} %bitcast.25, bf16[64,2048]{1,0:T(8,128)(2,1)} %bitcast.26, bf16[64,2048]{1,0:T(8,128)(2,1)} %bitcast.27, ...), custom_call_target="tpu_custom_call" | custom-call | flops 167772160 | bytes 1310720 | tf_op jit(solution)/shard_map/hidden/hidden/pallas_call | solution.py:193
  47.1 0.0 all-to-all-done.2.got
  47.1 1.0 %decode.1 = (f32[64,2048]{1,0:T(8,128)S(1)}, bf16[64,2048]{1,0:T(8,128)(2,1)S(1)}) custom-call(bf16[4,128,128]{2,1,0:T(8,128)(2,1)S(1)} %all-to-all-done.2.got, f32[128,2048]{1,0:T(8,128)S(1)} %get-tuple-element.12.partial, bf16[3,128,2048]{2,1,0:T(8,128)(2,1)S(1)} %slice_bitcast_fusion.dec), custom_call_target="tpu_custom_call" | custom-call | flops 201326592 | bytes 1572864 | tf_op jit(solution)/shard_map/decode/decode/pallas_call | solution.py:206
  48.1 2.2 %all-gather.1 = bf16[128,2048]{1,0:T(8,128)(2,1)S(1)} all-gather(bf16[64,2048]{1,0:T(8,128)(2,1)S(1)} %get-tuple-element.14), channel_id=3, replica_groups=mesh['layer'=4,'x_lo'=2,'core'=2,'z'=16,'x_hi'=2] {'core'}, dimensions={0}, use_global_device_ids=true | all-gather | bytes 786432 | tf_op jit(solution)/shard_map/reduce_core/all_gather | solution.py:217
  50.3 0.1 join.1
  50.4 9.6 %all_to_all.27 = bf16[4,16,16,128]{3,2,1,0:T(8,128)(2,1)S(1)} all-to-all(bf16[4,16,16,128]{3,2,1,0:T(8,128)(2,1)S(1)} %bitcast.22), channel_id=1, replica_groups=mesh['layer'=4,'x_lo'=2,'core'=2,'z'=16,'x_hi'=2] {'x_hi','x_lo'}, dimensions={0} | all-to-all | bytes 524288 | tf_op jit(solution)/shard_map/reduce_x/all_to_all | solution.py:228
  60.1 15.5 %all_to_all.28.got = bf16[16,16,128]{2,1,0:T(8,128)(2,1)S(1)} all-to-all(bf16[16,16,128]{2,1,0:T(8,128)(2,1)S(1)} %reduce_sum.12), channel_id=1, replica_groups={{16,18,20,22,24,26,28,30,0,2,4,6,8,10,12,14},{17,19,21,23,25,27,29,31,1..., dimensions={0} | all-to-all | bytes 131072 | tf_op jit(solution)/shard_map/reduce_z/all_to_all | solution.py:231
  75.7 0.7 last.1
  (3 shorter events, 0.1 us)
Async XLA Ops:
  0.6 36.2 %copy-start = (bf16[1,2048,128]{2,1,0:T(8,128)(2,1)S(1)}, bf16[1,2048,128]{2,1,0:T(8,128)(2,1)}, u32[]{:S(2)}) copy-start(bf16[1,2048,128]{2,1,0:T(8,128)(2,1)} %param.11) | copy-start | bytes 1572868
  38.5 8.6 %all-to-all-start.2 = ((bf16[4,128,128]{2,1,0:T(8,128)(2,1)}), bf16[4,128,128]{2,1,0:T(8,128)(2,1)S(1)}, u32[]{:S(2)}, u32[]{:S(2)}) async-start(bf16[4,128,128]{2,1,0:T(8,128)(2,1)} %get-tuple-element.9), calls=%async_computation.2 | async-start | bytes 262144 | tf_op jit(solution)/shard_map/exchange/all_to_all | solution.py:191
